TPU v7x, 32 devices: a whole 2x2x4 slice. The times are simulated.
32 devices in a mesh: wide: 8 (over z, y), narrow: 4 (over x, core).
Axes of the slice: x: 2, y: 2, z: 4, core: 2. Of those that a mesh axis runs over, the one named last changes fastest.
Arguments:
- features: bfloat16 [512, 32768], P('narrow', 'wide'), may hold values from -36 to 36
- edge_tiles: bfloat16 [256, 12, 128, 128], P('wide'), may hold values from 0 to 22, as said below
- block_lists: int32 [256, 12], P('wide'), may hold values from 0 to 47, as said below
- send_lists: int32 [8, 8, 2], P('wide'), may hold values from 0 to 31
- train_ids: int32 [2048], P('wide'), may hold values from 0 to 4095, as said below
- owners: int32 [2048, 1], P('wide'), may hold values from 0 to 31; in each aligned block of 256 rows (0 to 255, 256 to 511, ...) at most 16 rows name the same one
- cotangent: bfloat16 [4, 512, 2048], P(None, 'narrow', 'wide'), may hold values from -6 to 6
- query_weight: bfloat16 [512, 512], replicated, may hold values from -8 to 8
- key_weight: bfloat16 [512, 512], replicated, may hold values from -8 to 8
- value_weight: bfloat16 [512, 512], replicated, may hold values from -0.25 to 0.25
- out_weight: bfloat16 [512, 512], replicated, may hold values from -0.25 to 0.25
- up_weight: bfloat16 [2048, 512], replicated, may hold values from -0.25 to 0.25
- down_weight: bfloat16 [2048, 512], replicated, may hold values from -0.125 to 0.125
Outputs:
- hop_tokens: bfloat16 [3, 512, 32768], P(None, 'narrow', 'wide')
- grad_attn: float32 [2048, 512], P(('wide', 'narrow'))
- grad_up: float32 [2048, 512], P(('wide', 'narrow'))
- grad_down: float32 [2048, 512], P(('wide', 'narrow'))
Inputs may be any that keep to these rules, and one draw needn't show every extreme that they name: edge_tiles[b, k, s, t] weighs the edge from node s of block source[b, k] to node t of block b; the diagonal of every edge_tiles[b, 0] is positive. block_lists[b, 0] = b mod 32; within every part each position 32 to 47 appears. `train_ids`: distinct within a part. `owners`: at most 16 of the 256 training nodes of one part name the same owner; every owner is named by some node.
All inputs are finite; a program needn't handle non-finite values.
Results may differ from a plain program's by a relative error of at most 0.025.
Values may be sent and summed in bfloat16 or wider, within the bound.
A program may use at most 128 MiB of HBM per device.

v0:
```python
import math

import jax
import jax.numpy as jnp
from jax import lax
from jax.sharding import PartitionSpec as P

HEADS = 8
HOPS = 3
TOKS = 4


epsilon = 1e-05


def product_of(pattern, first_arg, second_arg):
    return jnp.einsum(pattern, first_arg, second_arg, preferred_element_type=jnp.float32)


def normalize(hidden):
    center = hidden - jnp.mean(hidden, axis=1, keepdims=True)
    inverse = lax.rsqrt(jnp.mean(center * center, axis=1, keepdims=True) + epsilon)
    return (center * inverse, inverse)


def norm_back(upstream, normed, inverse):
    return inverse * (
        upstream
        - jnp.mean(upstream, axis=1, keepdims=True)
        - normed * jnp.mean(upstream * normed, axis=1, keepdims=True)
    )


def gelu_tanh(values):
    return jax.nn.gelu(values, approximate=True)


def layer_grads(
    tokens, cotangent, query_weight, key_weight, value_weight, out_weight, up_weight, down_weight
):
    tok_count, feat_width, row_count = tokens.shape
    head_dim = feat_width // HEADS
    score_scale = 1.0 / math.sqrt(head_dim)
    split_heads = (tok_count, HEADS, head_dim, row_count)
    first_norm, _ = normalize(tokens.astype(jnp.float32))
    normed_a = first_norm.astype(jnp.bfloat16)
    query_heads = (
        product_of("od,tdr->tor", query_weight, normed_a).astype(jnp.bfloat16).reshape(split_heads)
    )
    key_heads = (
        product_of("od,tdr->tor", key_weight, normed_a).astype(jnp.bfloat16).reshape(split_heads)
    )
    value_heads = (
        product_of("od,tdr->tor", value_weight, normed_a).astype(jnp.bfloat16).reshape(split_heads)
    )
    scores = product_of("thdr,uhdr->htur", query_heads, key_heads) * score_scale
    attn_probs = jax.nn.softmax(scores, axis=2)
    attn_low = attn_probs.astype(jnp.bfloat16)
    mixed_heads = (
        product_of("htur,uhdr->thdr", attn_low, value_heads)
        .astype(jnp.bfloat16)
        .reshape(tok_count, feat_width, row_count)
    )
    residual = (
        tokens.astype(jnp.float32) + product_of("od,tdr->tor", out_weight, mixed_heads)
    ).astype(jnp.bfloat16)
    second_norm, second_inv = normalize(residual.astype(jnp.float32))
    normed_b = second_norm.astype(jnp.bfloat16)
    pre_act = product_of("fd,tdr->tfr", up_weight, normed_b)
    activated = gelu_tanh(pre_act).astype(jnp.bfloat16)
    sum_down = product_of("tfr,tdr->fd", activated, cotangent)
    grad_act = product_of("fd,tdr->tfr", down_weight, cotangent)
    _, gelu_back = jax.vjp(gelu_tanh, pre_act)
    grad_pre = gelu_back(grad_act)[0].astype(jnp.bfloat16)
    sum_up = product_of("tfr,tdr->fd", grad_pre, normed_b)
    grad_normed = product_of("fd,tfr->tdr", up_weight, grad_pre)
    grad_resid = (
        cotangent.astype(jnp.float32) + norm_back(grad_normed, second_norm, second_inv)
    ).astype(jnp.bfloat16)
    sum_out = product_of("tor,tdr->od", grad_resid, mixed_heads)
    grad_mixed = (
        product_of("od,tor->tdr", out_weight, grad_resid).astype(jnp.bfloat16).reshape(split_heads)
    )
    grad_probs = product_of("thdr,uhdr->htur", grad_mixed, value_heads)
    grad_value = product_of("htur,thdr->uhdr", attn_low, grad_mixed).astype(jnp.bfloat16)
    grad_scores = (
        attn_probs
        * (grad_probs - jnp.sum(attn_probs * grad_probs, axis=2, keepdims=True))
        * score_scale
    ).astype(jnp.bfloat16)
    grad_query = product_of("htur,uhdr->thdr", grad_scores, key_heads).astype(jnp.bfloat16)
    grad_key = product_of("htur,thdr->uhdr", grad_scores, query_heads).astype(jnp.bfloat16)
    flat_shape = (tok_count, feat_width, row_count)
    sum_query = product_of("tor,tdr->od", grad_query.reshape(flat_shape), normed_a)
    sum_key = product_of("tor,tdr->od", grad_key.reshape(flat_shape), normed_a)
    sum_value = product_of("tor,tdr->od", grad_value.reshape(flat_shape), normed_a)
    return (jnp.concatenate([sum_query, sum_key, sum_value, sum_out], axis=0), sum_up, sum_down)


def smooth_step(field, edge_tiles, block_lists, send_lists, degree):
    feat_width, node_count = field.shape
    count_blocks = block_lists.shape[0]
    blocks = field.reshape(feat_width, count_blocks, -1)
    outgoing = blocks[:, send_lists[0]]
    incoming = lax.all_to_all(outgoing, "wide", split_axis=1, concat_axis=1, tiled=True)
    block_pool = jnp.concatenate(
        [blocks, incoming.reshape(feat_width, -1, blocks.shape[2])], axis=1
    )
    picked = block_pool[:, block_lists]
    summed = product_of("dbks,bkst->dbt", picked, edge_tiles)
    return (summed / degree[None]).astype(jnp.bfloat16).reshape(feat_width, node_count)


def on_device(
    features,
    edge_tiles,
    block_lists,
    send_lists,
    train_ids,
    owners,
    cotangent,
    query_weight,
    key_weight,
    value_weight,
    out_weight,
    up_weight,
    down_weight,
):
    degree = jnp.sum(edge_tiles, axis=(1, 2), dtype=jnp.float32)
    current = features
    hop_list = []
    for hop_index in range(HOPS):
        applied_once = smooth_step(current, edge_tiles, block_lists, send_lists, degree)
        applied_twice = smooth_step(applied_once, edge_tiles, block_lists, send_lists, degree)
        current = (
            0.5 * current.astype(jnp.float32)
            + applied_once.astype(jnp.float32)
            + applied_twice.astype(jnp.float32)
        ).astype(jnp.bfloat16)
        hop_list.append(current)
    hop_tokens = jnp.stack(hop_list)
    everything = jnp.concatenate([features[None], hop_tokens], axis=0)
    width_local = features.shape[0]
    part_count = lax.axis_size("wide")
    narrow = lax.axis_size("narrow")
    devices = part_count * narrow
    train_rows = train_ids.shape[0]
    onehot = (owners == jnp.arange(devices, dtype=jnp.int32)[None]).astype(jnp.int32)
    counts = lax.psum(jnp.sum(onehot, axis=0), "wide")
    inverse = 1.0 / counts.astype(jnp.float32)
    row_scale = jnp.sum(onehot.astype(jnp.float32) * inverse[None], axis=1)
    scaled = (cotangent.astype(jnp.float32) * row_scale[None, None]).astype(jnp.bfloat16)
    row_share = train_rows // narrow
    own_tokens = everything[:, :, train_ids].reshape(TOKS, width_local, narrow, row_share)
    own_grads = scaled.reshape(TOKS, width_local, narrow, row_share)
    rows_in, grads_in = (
        lax.all_to_all(own_tokens, "narrow", split_axis=2, concat_axis=1, tiled=True),
        lax.all_to_all(own_grads, "narrow", split_axis=2, concat_axis=1, tiled=True),
    )
    full_width = width_local * narrow
    local_sums = layer_grads(
        rows_in.reshape(TOKS, full_width, -1),
        grads_in.reshape(TOKS, full_width, -1),
        query_weight,
        key_weight,
        value_weight,
        out_weight,
        up_weight,
        down_weight,
    )
    attn_part, up_part, down_part = local_sums
    grad_attn, grad_up, grad_down = (
        lax.psum_scatter(attn_part, ("wide", "narrow"), scatter_dimension=0, tiled=True),
        lax.psum_scatter(up_part, ("wide", "narrow"), scatter_dimension=0, tiled=True),
        lax.psum_scatter(down_part, ("wide", "narrow"), scatter_dimension=0, tiled=True),
    )
    return (hop_tokens, grad_attn, grad_up, grad_down)


def solution(mesh):
    in_specs = (
        P("narrow", "wide"),
        P("wide", None, None, None),
        P("wide", None),
        P("wide", None, None),
        P("wide"),
        P("wide", None),
        P(None, "narrow", "wide"),
        P(),
        P(),
        P(),
        P(),
        P(),
        P(),
    )
    out_specs = (
        P(None, "narrow", "wide"),
        P(("wide", "narrow"), None),
        P(("wide", "narrow"), None),
        P(("wide", "narrow"), None),
    )
    return jax.shard_map(
        on_device, mesh=mesh, in_specs=in_specs, out_specs=out_specs, check_vma=False
    )
```

profile of v0, /device:TPU:0, one launch (start us, length us, event | category | flops | bytes accessed | tf_op | source)
XLA Modules:
  0.0 891.5 jit_solution(1033297690688206011)
XLA Ops:
  21.0 7.4 convert_reduce_fusion
  37.7 12.7 %gather_fusion.1 = bf16[384,128,128]{2,1,0:T(8,128)(2,1)} fusion(bf16[128,48,128]{2,0,1:T(8,128)(2,1)} %pad_maximum_fusion.3, s32[1024]{0:T(1024)S(1)} %pad_clamp_fusion.1), kind=kCustom, calls=%fused_computation.1 | custom fusion | bytes 25167360 | tf_op jit(solution)/shard_map/gather | solution.py:109
  50.4 10.2 %fusion.24 = bf16[32,128,128]{1,2,0:T(8,128)(2,1)S(1)} fusion(bf16[128,32,12,128]{3,0,2,1:T(8,128)(2,1)} %bitcast.289, bf16[32,12,128,128]{3,2,1,0:T(8,128)(2,1)} %param.14, f32[32,128]{1,0:T(8,128)S(1)} %convert_reduce_fusion), kind=kOutput, calls=%fused_computation.53 | convolution fusion | flops 1611661312 | bytes 26230784 | tf_op jit(solution)/shard_map/dbks,bkst->dbt/dot_general | solution.py:17
  70.9 9.8 %all-to-all-done.1 = bf16[128,8,2,128]{0,3,2,1:T(8,128)(2,1)} async-done(((bf16[128,8,2,128]{0,3,2,1:T(8,128)(2,1)}), bf16[128,8,2,128]{0,3,2,1:T(8,128)(2,1)}, u32[]{:S(2)}, u32[]{:S(2)}) %all-to-all-start.1) | async-done | bytes 524320 | tf_op jit(solution)/shard_map/all_to_all | solution.py:105
  83.0 12.7 %gather_fusion.3 = bf16[384,128,128]{1,2,0:T(8,128)(2,1)} fusion(bf16[128,48,128]{0,2,1:T(8,128)(2,1)} %pad_maximum_fusion.4, s32[1024]{0:T(1024)S(1)} %pad_clamp_fusion.1), kind=kCustom, calls=%fused_computation.3 | custom fusion | bytes 25167360 | tf_op jit(solution)/shard_map/gather | solution.py:109
  95.7 16.6 %copy.232 = bf16[32,12,128,128]{3,2,1,0:T(8,128)(2,1)} copy(bf16[32,12,128,128]{2,3,1,0:T(8,128)(2,1)} %bitcast.283) | data formatting | bytes 25165824 | tf_op jit(solution)/shard_map/gather | solution.py:109
  112.4 11.5 %fusion.33 = f32[32,128,128]{1,2,0:T(8,128)} fusion(bf16[32,12,128,128]{3,2,1,0:T(8,128)(2,1)} %param.14, bf16[32,12,128,128]{3,2,1,0:T(8,128)(2,1)} %copy.232, f32[32,128]{1,0:T(8,128)S(1)} %convert_reduce_fusion), kind=kOutput, calls=%fused_computation.64 | convolution fusion | flops 1612185600 | bytes 27279360 | tf_op jit(solution)/shard_map/dbks,bkst->dbt/dot_general | solution.py:17
  135.9 18.2 %all_to_all.54 = bf16[128,8,2,128]{3,0,2,1:T(8,128)(2,1)S(1)} all-to-all(bf16[128,8,2,128]{3,0,2,1:T(8,128)(2,1)} %bitcast.310), channel_id=1, replica_groups=mesh['wide'=8,'narrow'=4] {'wide'}, dimensions={1} | all-to-all | bytes 1048576 | tf_op jit(solution)/shard_map/all_to_all | solution.py:105
  156.6 12.7 %gather_fusion.5 = bf16[384,128,128]{2,1,0:T(8,128)(2,1)} fusion(bf16[128,48,128]{2,0,1:T(8,128)(2,1)} %pad_maximum_fusion.5, s32[1024]{0:T(1024)S(1)} %pad_clamp_fusion.1), kind=kCustom, calls=%fused_computation.5 | custom fusion | bytes 25167360 | tf_op jit(solution)/shard_map/gather | solution.py:109
  169.3 11.2 %fusion.22 = bf16[32,128,128]{1,2,0:T(8,128)(2,1)} fusion(bf16[128,32,12,128]{3,0,2,1:T(8,128)(2,1)} %bitcast.290, bf16[32,12,128,128]{3,2,1,0:T(8,128)(2,1)} %param.14, f32[32,128]{1,0:T(8,128)S(1)} %convert_reduce_fusion), kind=kOutput, calls=%fused_computation.49 | convolution fusion | flops 1611661312 | bytes 26230784 | tf_op jit(solution)/shard_map/dbks,bkst->dbt/dot_general | solution.py:17
  193.4 8.1 all-to-all-done.3
  204.1 12.7 %gather_fusion.7 = bf16[384,128,128]{1,2,0:T(8,128)(2,1)} fusion(bf16[128,48,128]{0,2,1:T(8,128)(2,1)} %pad_maximum_fusion.6, s32[1024]{0:T(1024)S(1)} %pad_clamp_fusion.1), kind=kCustom, calls=%fused_computation.7 | custom fusion | bytes 25167360 | tf_op jit(solution)/shard_map/gather | solution.py:109
  216.8 16.6 %copy.240 = bf16[32,12,128,128]{3,2,1,0:T(8,128)(2,1)} copy(bf16[32,12,128,128]{2,3,1,0:T(8,128)(2,1)} %bitcast.284) | data formatting | bytes 25165824 | tf_op jit(solution)/shard_map/gather | solution.py:109
  233.5 11.5 %fusion.36 = f32[32,128,128]{1,2,0:T(8,128)} fusion(bf16[32,12,128,128]{3,2,1,0:T(8,128)(2,1)} %param.14, bf16[32,12,128,128]{3,2,1,0:T(8,128)(2,1)} %copy.240, f32[32,128]{1,0:T(8,128)S(1)} %convert_reduce_fusion), kind=kOutput, calls=%fused_computation.65 | convolution fusion | flops 1612185600 | bytes 27279360 | tf_op jit(solution)/shard_map/dbks,bkst->dbt/dot_general | solution.py:17
  269.6 11.8 %psum.7 = s32[32]{0:T(128)S(1)} all-reduce(s32[32]{0:T(128)S(1)} %convert_reduce_fusion.1), channel_id=1, replica_groups=mesh['wide'=8,'narrow'=4] {'wide'}, use_global_device_ids=true, to_apply=%region_6.0 | all-reduce | flops 32 | bytes 256 | tf_op jit(solution)/shard_map/psum | solution.py:149
  294.4 12.7 %gather_fusion.9 = bf16[384,128,128]{2,1,0:T(8,128)(2,1)} fusion(bf16[128,48,128]{2,0,1:T(8,128)(2,1)} %pad_maximum_fusion.7, s32[1024]{0:T(1024)S(1)} %pad_clamp_fusion.1), kind=kCustom, calls=%fused_computation.9 | custom fusion | bytes 25167360 | tf_op jit(solution)/shard_map/gather | solution.py:109
  307.1 11.2 %fusion.20 = bf16[32,128,128]{1,2,0:T(8,128)(2,1)} fusion(bf16[128,32,12,128]{3,0,2,1:T(8,128)(2,1)} %bitcast.291, bf16[32,12,128,128]{3,2,1,0:T(8,128)(2,1)} %param.14, f32[32,128]{1,0:T(8,128)S(1)} %convert_reduce_fusion), kind=kOutput, calls=%fused_computation.45 | convolution fusion | flops 1611661312 | bytes 26230784 | tf_op jit(solution)/shard_map/dbks,bkst->dbt/dot_general | solution.py:17
  341.9 12.7 %gather_fusion.11 = bf16[384,128,128]{1,2,0:T(8,128)(2,1)} fusion(bf16[128,48,128]{0,2,1:T(8,128)(2,1)} %pad_maximum_fusion.8, s32[1024]{0:T(1024)S(1)} %pad_clamp_fusion.1), kind=kCustom, calls=%fused_computation.11 | custom fusion | bytes 25167360 | tf_op jit(solution)/shard_map/gather | solution.py:109
  354.7 16.6 %copy.248 = bf16[32,12,128,128]{3,2,1,0:T(8,128)(2,1)} copy(bf16[32,12,128,128]{2,3,1,0:T(8,128)(2,1)} %bitcast.282) | data formatting | bytes 25165824 | tf_op jit(solution)/shard_map/gather | solution.py:109
  371.3 11.5 %fusion.39 = f32[32,128,128]{1,2,0:T(8,128)} fusion(bf16[32,12,128,128]{3,2,1,0:T(8,128)(2,1)} %param.14, bf16[32,12,128,128]{3,2,1,0:T(8,128)(2,1)} %copy.248, f32[32,128]{1,0:T(8,128)S(1)} %convert_reduce_fusion), kind=kOutput, calls=%fused_computation.66 | convolution fusion | flops 1612185600 | bytes 27279360 | tf_op jit(solution)/shard_map/dbks,bkst->dbt/dot_general | solution.py:17
  395.2 12.3 %pad_maximum_fusion = bf16[4,128,4096]{1,0,2:T(4,128)(2,1)} fusion(bf16[1,128,4096]{1,0,2:T(2,128)(2,1)} %copy.254, bf16[1,128,4096]{1,0,2:T(2,128)(2,1)} %copy.253, bf16[1,128,4096]{1,0,2:T(2,128)(2,1)} %copy.252, bf16[1,128,4096]{1,0,2:T(2,128)(2,1)} %copy.251), kind=kLoop, calls=%fused_computation.22 | loop fusion | flops 16777216 | bytes 8388608 | tf_op jit(solution)/shard_map/concatenate | solution.py:142
  510.2 91.1 %reduce-scatter.6.cloned.1.call-done = f32[64,512]{1,0:T(8,128)} async-done(((f32[2048,512]{1,0:T(8,128)}), f32[64,512]{1,0:T(8,128)}) %reduce-scatter.6.cloned.1.call-update) | async-done | bytes 131088 | tf_op jit(solution)/shard_map/reduce_scatter | solution.py:174
  601.3 141.9 %reduce-scatter.4.cloned.1.call-done = f32[64,512]{1,0:T(8,128)} async-done(((f32[2048,512]{1,0:T(8,128)}), f32[64,512]{1,0:T(8,128)}) %reduce-scatter.4.cloned.1.call-update) | async-done | bytes 131088 | tf_op jit(solution)/shard_map/reduce_scatter | solution.py:173
  743.1 141.4 %reduce-scatter.8.cloned.1.call-done = f32[64,512]{1,0:T(8,128)} async-done(((f32[2048,512]{1,0:T(8,128)}), f32[64,512]{1,0:T(8,128)}) %reduce-scatter.8.cloned.1.call-update) | async-done | bytes 131088 | tf_op jit(solution)/shard_map/reduce_scatter | solution.py:175
  (153 shorter events, 241.6 us)
Async XLA Ops:
  7.2 446.0 %copy-start = (bf16[2048,512]{1,0:T(8,128)(2,1)S(1)}, bf16[2048,512]{1,0:T(8,128)(2,1)}, u32[]{:S(2)}) copy-start(bf16[2048,512]{1,0:T(8,128)(2,1)} %param.24) | copy-start | bytes 6291460
  10.4 10.4 %copy-start.12 = (s32[32,12]{0,1:T(8,128)S(1)}, s32[32,12]{0,1:T(8,128)}, u32[]{:S(2)}) copy-start(s32[32,12]{0,1:T(8,128)} %param.15) | copy-start | bytes 4612
  13.5 21.9 %all-to-all-start = ((bf16[128,8,2,128]{3,0,2,1:T(8,128)(2,1)}), bf16[128,8,2,128]{3,0,2,1:T(8,128)(2,1)}, u32[]{:S(2)}, u32[]{:S(2)}) async-start(bf16[128,8,2,128]{3,0,2,1:T(8,128)(2,1)} %bitcast.306), calls=%async_computation | async-start | bytes 1048576 | tf_op jit(solution)/shard_map/all_to_all | solution.py:105
  62.1 18.6 %all-to-all-start.1 = ((bf16[128,8,2,128]{0,3,2,1:T(8,128)(2,1)}), bf16[128,8,2,128]{0,3,2,1:T(8,128)(2,1)}, u32[]{:S(2)}, u32[]{:S(2)}) async-start(bf16[128,8,2,128]{0,3,2,1:T(8,128)(2,1)} %bitcast.308), calls=%async_computation.1 | async-start | bytes 1048576 | tf_op jit(solution)/shard_map/all_to_all | solution.py:105
  183.2 18.3 %all-to-all-start.3 = ((bf16[128,8,2,128]{0,3,2,1:T(8,128)(2,1)}), bf16[128,8,2,128]{0,3,2,1:T(8,128)(2,1)}, u32[]{:S(2)}, u32[]{:S(2)}) async-start(bf16[128,8,2,128]{0,3,2,1:T(8,128)(2,1)} %bitcast.309), calls=%async_computation.3 | async-start | bytes 1048576 | tf_op jit(solution)/shard_map/all_to_all | solution.py:105
  253.7 9.1 %copy-start.13 = (s32[256,1]{0,1:T(1,128)S(1)}, s32[256,1]{0,1:T(1,128)}, u32[]{:S(2)}) copy-start(s32[256,1]{0,1:T(1,128)} %param.18) | copy-start | bytes 3076
  258.7 33.1 %all-to-all-start.4 = ((bf16[128,8,2,128]{3,0,2,1:T(8,128)(2,1)}), bf16[128,8,2,128]{3,0,2,1:T(8,128)(2,1)}, u32[]{:S(2)}, u32[]{:S(2)}) async-start(bf16[128,8,2,128]{3,0,2,1:T(8,128)(2,1)} %bitcast.305), calls=%async_computation.4 | async-start | bytes 1048576 | tf_op jit(solution)/shard_map/all_to_all | solution.py:105
  262.9 19.4 %copy-start.14 = (s32[256]{0:T(256)S(1)}, s32[256]{0:T(256)}, u32[]{:S(2)}) copy-start(s32[256]{0:T(256)} %param.17) | copy-start | bytes 3076
  321.0 14.7 %all-to-all-start.5 = ((bf16[128,8,2,128]{0,3,2,1:T(8,128)(2,1)}), bf16[128,8,2,128]{0,3,2,1:T(8,128)(2,1)}, u32[]{:S(2)}, u32[]{:S(2)}) async-start(bf16[128,8,2,128]{0,3,2,1:T(8,128)(2,1)} %bitcast.307), calls=%async_computation.5 | async-start | bytes 1048576 | tf_op jit(solution)/shard_map/all_to_all | solution.py:105
  335.7 77.3 %all-to-all-start.7 = ((bf16[4,128,4,64]{1,3,0,2:T(8,128)(2,1)}), bf16[4,128,4,64]{1,3,0,2:T(8,128)(2,1)S(1)}, u32[]{:S(2)}, u32[]{:S(2)}) async-start(bf16[4,128,4,64]{1,3,0,2:T(8,128)(2,1)} %copy.261), calls=%async_computation.7 | async-start | bytes 524288 | tf_op jit(solution)/shard_map/all_to_all | solution.py:158
  413.7 9.4 %all-to-all-start.6 = ((bf16[4,128,4,64]{1,3,0,2:T(8,128)(2,1)}), bf16[4,128,4,64]{1,3,0,2:T(8,128)(2,1)S(1)}, u32[]{:S(2)}, u32[]{:S(2)}) async-start(bf16[4,128,4,64]{1,3,0,2:T(8,128)(2,1)} %copy.256), calls=%async_computation.6 | async-start | bytes 524288 | tf_op jit(solution)/shard_map/all_to_all | solution.py:157
  417.1 184.1 %reduce-scatter.6.cloned.1.call-start = ((), (), s32[]{:S(2)}) async-start(), calls=%async_computation.12 | async-start | bytes 4325376 | tf_op jit(solution)/shard_map/reduce_scatter | solution.py:174
  452.9 3.7 copy-start.1
  453.2 1.0 copy-start.9
  453.2 1.7 copy-start.15
  454.9 1.8 copy-start.4
  456.6 1.0 copy-start.16
  460.4 282.7 %reduce-scatter.4.cloned.1.call-start = ((), (), s32[]{:S(2)}) async-start(), calls=%async_computation.11 | async-start | bytes 4325376 | tf_op jit(solution)/shard_map/reduce_scatter | solution.py:173
  460.7 2.3 copy-start.2
  460.7 2.3 copy-start.10
  460.7 3.3 copy-start.5
  495.3 2.7 copy-start.7
  495.3 3.0 copy-start.8
  501.1 383.4 %reduce-scatter.8.cloned.1.call-start = ((), (), s32[]{:S(2)}) async-start(), calls=%async_computation.13 | async-start | bytes 4325376 | tf_op jit(solution)/shard_map/reduce_scatter | solution.py:175
  (3 other events, 2.4 us)
Sparse Core Ops, SparseCore 0:
  460.5 140.6 reduce-scatter.5
  604.1 138.9 reduce-scatter.3
  746.0 138.5 reduce-scatter.7
where the time goes:
time: 903 us; the launch traced here: 892 us
  waiting for transfers between devices  406 us (45%)
  local copies, waits for them, and re-layouts  232 us (26%)
  matrix products  116 us (13%)
  other arithmetic  61.2 us (7%)
  starting transfers between devices  32.1 us (4%)
  blocking collectives  30 us (3%)
  between operations  14.6 us (2%)
    reduce_scatter x1, waiting for transfers between devices, on_device(): lax.psum_scatter(attn_part, ('wide', 'narrow'), scatter_dimension=0, tile...  142 us
    reduce_scatter x1, waiting for transfers between devices, on_device(): lax.psum_scatter(down_part, ('wide', 'narrow'), scatter_dimension=0, tile...  141 us
    gather x9, local copies, waits for them, and re-layouts, smooth_step(): picked = block_pool[:, block_lists]  126 us
    dot_general x25, matrix products, product_of(): jnp.einsum(pattern, first_arg, second_arg, preferred_element_type=jnp.flo...  111 us
    reduce_scatter x1, waiting for transfers between devices, on_device(): lax.psum_scatter(up_part, ('wide', 'narrow'), scatter_dimension=0, tiled=...  91.1 us
    all_to_all x5, waiting for transfers between devices, smooth_step(): lax.all_to_all(outgoing, 'wide', split_axis=1, concat_axis=1, tiled=True)  29.8 us
    all_to_all x5, starting transfers between devices, smooth_step(): lax.all_to_all(outgoing, 'wide', split_axis=1, concat_axis=1, tiled=True)  24.5 us
    all_to_all x1, blocking collectives, smooth_step(): lax.all_to_all(outgoing, 'wide', split_axis=1, concat_axis=1, tiled=True)  18.2 us
  transfers between devices with their start and end apart: 10, of which 8 were waited for; matrix products, arithmetic and copies ran while one was open for 19% of the time, Pallas kernels for 0%

commit v1 on v0

v1 whole, which is shorter than its diff:
```python
import functools
import math

import jax
import jax.numpy as jnp
from jax import lax
from jax.experimental import pallas as pl
from jax.experimental.pallas import tpu as pltpu
from jax.sharding import PartitionSpec as P

HEADS = 8
HOPS = 3
TOKS = 4
EPSILON = 1e-05
LANES = 128
MESH = pl.DeviceIdType.MESH
NT = (((1,), (1,)), ((), ()))
TN = (((0,), (0,)), ((), ()))
NN = (((1,), (0,)), ((), ()))
f32 = jnp.float32
bf16 = jnp.bfloat16


def dot(a, b, dims=NN):
    return lax.dot_general(a, b, dims, preferred_element_type=f32)


def hop_kernel(
    parts, lists, sends, feat, tiles_hbm, ids, cnt,
    hops_out, picked_out, cnt_out,
    pool_a, pool_b, fresh, tiles, degree, stage, onehot, cnt_buf,
    tile_sem, send_sem, recv_sem, cnt_send, cnt_recv,
):
    me = lax.axis_index("wide")
    blocks, fan = lists.shape
    slots = sends.shape[2]
    width = feat.shape[0]

    load = pltpu.make_async_copy(tiles_hbm, tiles, tile_sem)
    load.start()

    barrier = pltpu.get_barrier_semaphore()

    @pl.loop(1, parts)
    def _(d):
        peer = lax.rem(me + d, parts)
        pl.semaphore_signal(barrier, inc=1, device_id={"wide": peer}, device_id_type=MESH)

    for b in range(blocks):
        block = feat[:, b * LANES:(b + 1) * LANES]
        pool_a[b] = block
        fresh[b] = block
    pl.semaphore_wait(barrier, parts - 1)

    def halo_copy(pool, parity, dst, src):
        return pltpu.make_async_remote_copy(
            src_ref=stage.at[dst],
            dst_ref=pool.at[pl.ds(blocks + src * slots, slots)],
            send_sem=send_sem.at[dst],
            recv_sem=recv_sem.at[parity, src],
            device_id={"wide": dst},
            device_id_type=MESH,
        )

    def count_copy(dst, src):
        return pltpu.make_async_remote_copy(
            src_ref=cnt,
            dst_ref=cnt_buf.at[src],
            send_sem=cnt_send.at[dst],
            recv_sem=cnt_recv.at[src],
            device_id={"wide": dst},
            device_id_type=MESH,
        )

    def start_halo(pool, parity):
        @pl.loop(1, parts)
        def _(d):
            peer = lax.rem(me + d, parts)
            for q in range(slots):
                stage[peer, q] = fresh[sends[0, peer, q]]
            halo_copy(pool, parity, peer, me).start()

        for q in range(slots):
            pool[blocks + me * slots + q] = fresh[sends[0, me, q]]

    def finish_halo(pool, parity):
        @pl.loop(1, parts)
        def _(d):
            peer = lax.rem(me + d, parts)
            halo_copy(pool, parity, me, peer).wait_recv()

        @pl.loop(1, parts)
        def _(d):
            peer = lax.rem(me + d, parts)
            halo_copy(pool, parity, peer, me).wait_send()

    def apply(pool, b):
        left = jnp.concatenate([pool[lists[b, k]] for k in range(fan)], axis=1)
        summed = dot(left, tiles[b])
        return (summed / degree[pl.ds(b, 1), :]).astype(bf16)

    start_halo(pool_a, 0)

    @pl.loop(1, parts)
    def _(d):
        peer = lax.rem(me + d, parts)
        count_copy(peer, me).start()

    node_count = onehot.shape[0]
    step = node_count // blocks

    @pl.loop(0, blocks)
    def _(b):
        start = pl.multiple_of(b * step, step)
        rows = lax.broadcasted_iota(jnp.int32, (step, onehot.shape[1]), 0) + start
        onehot[pl.ds(start, step), :] = jnp.where(rows == ids[...], 1.0, 0.0).astype(bf16)

    picked_out[0] = dot(feat[...], onehot[...]).astype(bf16)
    load.wait()

    @pl.loop(0, blocks)
    def _(b):
        degree[pl.ds(b, 1), :] = jnp.sum(tiles[b].astype(f32), axis=0, keepdims=True)

    @pl.loop(0, HOPS)
    def _(hop):
        finish_halo(pool_a, 0)

        @pl.loop(0, blocks, step=2)
        def _(b):
            for c in range(2):
                once = apply(pool_a, b + c)
                pool_b[b + c] = once
                fresh[b + c] = once

        start_halo(pool_b, 1)
        finish_halo(pool_b, 1)

        @pl.loop(0, blocks, step=2)
        def _(b):
            for c in range(2):
                twice = apply(pool_b, b + c).astype(f32)
                smooth = 0.5 * pool_a[b + c].astype(f32) + pool_b[b + c].astype(f32) + twice
                smooth = smooth.astype(bf16)
                pool_a[b + c] = smooth
                fresh[b + c] = smooth
                start = pl.multiple_of((b + c) * LANES, LANES)
                hops_out[hop, :, pl.ds(start, LANES)] = smooth

        @pl.when(hop < HOPS - 1)
        def _():
            start_halo(pool_a, 0)

        picked_out[hop + 1] = dot(hops_out[hop], onehot[...]).astype(bf16)

    cnt_buf[me] = cnt[...]

    @pl.loop(1, parts)
    def _(d):
        peer = lax.rem(me + d, parts)
        count_copy(me, peer).wait_recv()

    @pl.loop(1, parts)
    def _(d):
        peer = lax.rem(me + d, parts)
        count_copy(peer, me).wait_send()

    cnt_out[...] = jnp.sum(cnt_buf[...], axis=0)


def smooth_hops(features, edge_tiles, block_lists, send_lists, train_ids, counts):
    width, nodes = features.shape
    blocks, fan, size, _ = edge_tiles.shape
    parts, slots = send_lists.shape[1:]
    rows = train_ids.shape[0]
    halo = parts * slots
    vmem = pl.BlockSpec(memory_space=pltpu.VMEM)
    smem = pl.BlockSpec(memory_space=pltpu.SMEM)
    return pl.pallas_call(
        functools.partial(hop_kernel, parts),
        out_shape=(
            jax.ShapeDtypeStruct((HOPS, width, nodes), bf16),
            jax.ShapeDtypeStruct((TOKS, width, rows), bf16),
            jax.ShapeDtypeStruct(counts.shape, f32),
        ),
        in_specs=[smem, smem, vmem, pl.BlockSpec(memory_space=pl.ANY), vmem, vmem],
        out_specs=(vmem, vmem, vmem),
        scratch_shapes=[
            pltpu.VMEM((blocks + halo, width, size), bf16),
            pltpu.VMEM((blocks + halo, width, size), bf16),
            pltpu.VMEM((blocks, width, size), bf16),
            pltpu.VMEM((blocks, fan * size, size), bf16),
            pltpu.VMEM((blocks, size), f32),
            pltpu.VMEM((parts, slots, width, size), bf16),
            pltpu.VMEM((nodes, rows), bf16),
            pltpu.VMEM((parts,) + counts.shape, f32),
            pltpu.SemaphoreType.DMA,
            pltpu.SemaphoreType.DMA((parts,)),
            pltpu.SemaphoreType.DMA((2, parts)),
            pltpu.SemaphoreType.DMA((parts,)),
            pltpu.SemaphoreType.DMA((parts,)),
        ],
        compiler_params=pltpu.CompilerParams(
            collective_id=0, has_side_effects=True, vmem_limit_bytes=56 * 2**20
        ),
        name="smooth_hops",
    )(
        block_lists, send_lists, features,
        edge_tiles.reshape(blocks, fan * size, size),
        train_ids.reshape(1, rows), counts,
    )


def normalize(hidden):
    center = hidden - jnp.mean(hidden, axis=0, keepdims=True)
    inverse = lax.rsqrt(jnp.mean(center * center, axis=0, keepdims=True) + EPSILON)
    return center * inverse, inverse


def layer_kernel(
    packed, wq, wk, wv, wo, wu, wd, attn_out, up_out, down_out, nb_ref, cot_ref, g_ref
):
    share = packed.shape[2]
    width = packed.shape[1]
    cols = TOKS * share
    head = width // HEADS
    scale = 1.0 / math.sqrt(head)
    x = jnp.concatenate([packed[t].astype(f32) for t in range(TOKS)], axis=1)
    cot32 = jnp.concatenate([packed[TOKS + t].astype(f32) for t in range(TOKS)], axis=1)
    cot_ref[...] = cot32.astype(bf16)

    def ahead(v, j):
        return v if j == 0 else pltpu.roll(v, cols - j * share, 1)

    def back(v, j):
        return v if j == 0 else pltpu.roll(v, j * share, 1)

    def head_sum(v):
        return jnp.sum(v.reshape(HEADS, head, cols), axis=1)

    def spread(v):
        return jnp.broadcast_to(v[:, None, :], (HEADS, head, cols)).reshape(width, cols)

    def low(v):
        return v.astype(bf16).astype(f32)

    normed_a = normalize(x)[0].astype(bf16)
    query = low(dot(wq[...], normed_a))
    key = low(dot(wk[...], normed_a))
    value = low(dot(wv[...], normed_a))
    scores = [head_sum(query * ahead(key, j)) * scale for j in range(TOKS)]
    top = functools.reduce(jnp.maximum, scores)
    exps = [jnp.exp(s - top) for s in scores]
    total = functools.reduce(jnp.add, exps)
    probs = [e / total for e in exps]
    probs_low = [low(p) for p in probs]
    mixed = functools.reduce(
        jnp.add, [spread(probs_low[j]) * ahead(value, j) for j in range(TOKS)]
    ).astype(bf16)
    residual = low(x + dot(wo[...], mixed))
    second, inverse = normalize(residual)
    nb_ref[...] = second.astype(bf16)
    g_ref[...] = jnp.zeros_like(g_ref)
    chunk = 256
    slope = math.sqrt(2.0 / math.pi)

    @pl.loop(0, wu.shape[0] // chunk)
    def _(i):
        rows = pl.ds(pl.multiple_of(i * chunk, chunk), chunk)
        up = wu[rows, :]
        cot = cot_ref[...]
        normed_b = nb_ref[...]
        pre = dot(up, normed_b)
        square = pre * pre
        tanh = jnp.tanh(slope * (pre + 0.044715 * (square * pre)))
        activated = (0.5 * pre * (1.0 + tanh)).astype(bf16)
        deriv = 0.5 * (1.0 + tanh) + 0.5 * pre * (1.0 - tanh * tanh) * (
            slope * (1.0 + 3.0 * 0.044715 * square)
        )
        down_out[rows, :] = dot(activated, cot, NT).astype(bf16)
        grad_pre = (dot(wd[rows, :], cot) * deriv).astype(bf16)
        up_out[rows, :] = dot(grad_pre, normed_b, NT).astype(bf16)
        g_ref[...] += dot(up, grad_pre, TN)

    upstream = g_ref[...]
    grad_resid = (
        cot32
        + inverse
        * (
            upstream
            - jnp.mean(upstream, axis=0, keepdims=True)
            - second * jnp.mean(upstream * second, axis=0, keepdims=True)
        )
    ).astype(bf16)
    attn_out[3 * width:4 * width, :] = dot(grad_resid, mixed, NT).astype(bf16)
    grad_mixed = low(dot(wo[...], grad_resid, TN))
    grad_probs = [head_sum(grad_mixed * ahead(value, j)) for j in range(TOKS)]
    grad_value = functools.reduce(
        jnp.add, [back(spread(probs_low[j]) * grad_mixed, j) for j in range(TOKS)]
    ).astype(bf16)
    attn_out[2 * width:3 * width, :] = dot(grad_value, normed_a, NT).astype(bf16)
    inner = functools.reduce(jnp.add, [p * g for p, g in zip(probs, grad_probs)])
    grad_scores = [low(p * (g - inner) * scale) for p, g in zip(probs, grad_probs)]
    grad_query = functools.reduce(
        jnp.add, [spread(grad_scores[j]) * ahead(key, j) for j in range(TOKS)]
    ).astype(bf16)
    attn_out[0:width, :] = dot(grad_query, normed_a, NT).astype(bf16)
    grad_key = functools.reduce(
        jnp.add, [back(spread(grad_scores[j]) * query, j) for j in range(TOKS)]
    ).astype(bf16)
    attn_out[width:2 * width, :] = dot(grad_key, normed_a, NT).astype(bf16)


def layer_sums(packed, wq, wk, wv, wo, wu, wd):
    width = packed.shape[1]
    cols = TOKS * packed.shape[2]
    vmem = pl.BlockSpec(memory_space=pltpu.VMEM)
    return pl.pallas_call(
        layer_kernel,
        out_shape=(
            jax.ShapeDtypeStruct((4 * width, width), bf16),
            jax.ShapeDtypeStruct(wu.shape, bf16),
            jax.ShapeDtypeStruct(wd.shape, bf16),
        ),
        in_specs=[vmem] * 7,
        out_specs=(vmem, vmem, vmem),
        scratch_shapes=[
            pltpu.VMEM((width, cols), bf16),
            pltpu.VMEM((width, cols), bf16),
            pltpu.VMEM((width, cols), f32),
        ],
        compiler_params=pltpu.CompilerParams(vmem_limit_bytes=48 * 2**20),
        name="layer_sums",
    )(packed, wq, wk, wv, wo, wu, wd)


def halving_sum(term, bits, order):
    count = len(bits)
    depth = term.shape[1]
    term = term.reshape((2,) * count + (-1, depth))
    left = list(range(count))
    for place, bit in enumerate(order):
        axis, shift = bits[bit]
        size = lax.axis_size(axis)
        mine = lax.rem(lax.axis_index(axis) // (1 << shift), 2)
        dim = left.index(bit)
        left.remove(bit)
        sent = lax.dynamic_index_in_dim(term, 1 - mine, dim, keepdims=False)
        kept = lax.dynamic_index_in_dim(term, mine, dim, keepdims=False)
        got = lax.ppermute(sent, axis, [(i, i ^ (1 << shift)) for i in range(size)])
        term = kept.astype(f32) + got.astype(f32)
        if place < count - 1:
            term = term.astype(bf16)
    return term


def on_device(
    features, edge_tiles, block_lists, send_lists, train_ids, owners, cotangent,
    query_weight, key_weight, value_weight, out_weight, up_weight, down_weight,
):
    parts = lax.axis_size("wide")
    narrow = lax.axis_size("narrow")
    devices = parts * narrow
    rows = train_ids.shape[0]
    share = rows // narrow
    width = features.shape[0]
    padded = -(-devices // LANES) * LANES
    onehot = (owners == jnp.arange(padded, dtype=jnp.int32)[None]).astype(f32)
    own_counts = jnp.broadcast_to(jnp.sum(onehot, axis=0)[None], (8, padded))
    hop_tokens, picked, counts = smooth_hops(
        features, edge_tiles, block_lists, send_lists, train_ids, own_counts
    )
    inverse = 1.0 / jnp.maximum(counts[0], 1.0)
    row_scale = jnp.sum(onehot * inverse[None], axis=1)
    scaled = (cotangent.astype(f32) * row_scale[None, None]).astype(bf16)
    packed = jnp.concatenate([picked, scaled], axis=0).reshape(2 * TOKS, width, narrow, share)
    packed = lax.all_to_all(packed, "narrow", split_axis=2, concat_axis=1, tiled=True)
    packed = packed.reshape(2 * TOKS, width * narrow, share)
    attn_part, up_part, down_part = layer_sums(
        packed, query_weight, key_weight, value_weight, out_weight, up_weight, down_weight
    )
    bits = [("wide", s) for s in reversed(range(parts.bit_length() - 1))]
    wide_bits = list(range(len(bits)))
    bits += [("narrow", s) for s in reversed(range(narrow.bit_length() - 1))]
    narrow_bits = list(range(len(wide_bits), len(bits)))
    core, across = narrow_bits[-1], narrow_bits[:-1][::-1]
    low_wide, high_wide = wide_bits[-1:], wide_bits[:-1][::-1]
    orders = (
        [core] + across + low_wide + high_wide,
        [core] + low_wide + high_wide + across,
        [core] + high_wide + across + low_wide,
    )
    return (
        hop_tokens,
        halving_sum(attn_part, bits, orders[0]),
        halving_sum(up_part, bits, orders[1]),
        halving_sum(down_part, bits, orders[2]),
    )


def solution(mesh):
    in_specs = (
        P("narrow", "wide"),
        P("wide", None, None, None),
        P("wide", None),
        P("wide", None, None),
        P("wide"),
        P("wide", None),
        P(None, "narrow", "wide"),
        P(),
        P(),
        P(),
        P(),
        P(),
        P(),
    )
    out_specs = (
        P(None, "narrow", "wide"),
        P(("wide", "narrow"), None),
        P(("wide", "narrow"), None),
        P(("wide", "narrow"), None),
    )
    return jax.shard_map(
        on_device, mesh=mesh, in_specs=in_specs, out_specs=out_specs, check_vma=False
    )
```

time: 903 us -> 204 us (0.23); the launches traced: 892 us -> 203 us
  waiting for transfers between devices: 406 us -> 27.9 us
  local copies, waits for them, and re-layouts: 232 us -> 13.9 us
  Pallas kernels: 0 us -> 123 us
  matrix products: 116 us -> 0 us
  other arithmetic: 61.2 us -> 10.1 us
  blocking collectives: 30 us -> 0 us
  between operations: 14.6 us -> 0.97 us
    reduce_scatter x3 -> x0, waiting for transfers between devices: 374 us -> none  [the longest x1 142 us: on_device(): lax.psum_scatter(attn_part, ('wide', 'narrow'), scatter_dimension=0, tile...]
    gather x16 -> x0, local copies, waits for them, and re-layouts: 143 us -> none  [the longest x9 126 us: smooth_step(): picked = block_pool[:, block_lists]]
    pallas_call x0 -> x2, Pallas kernels: none -> 123 us  [the longest x1 112 us: smooth_hops(): pl.pallas_call(functools.partial(hop_kernel, parts), out_shape=(jax.Shape...]
    dot_general x25 -> x0, matrix products: 111 us -> none  [product_of(): jnp.einsum(pattern, first_arg, second_arg, preferred_element_type=jnp.flo...]
    convert_element_type x14 -> x0, local copies, waits for them, and re-layouts: 30.9 us -> none  [the longest x3 8.78 us: on_device(): applied_once.astype(jnp.float32)]
    concatenate x8 -> x1, other arithmetic: 29.9 us -> 1 us  [on_device(): jnp.concatenate([picked, scaled], axis=0)]
    all_to_all x7 -> x1, starting transfers between devices: 31.5 us -> 3.47 us  [on_device(): lax.all_to_all(packed, 'narrow', split_axis=2, concat_axis=1, tiled=True)]
    reshape x14 -> x1, local copies, waits for them, and re-layouts: 27 us -> 0.84 us  [on_device(): jnp.concatenate([picked, scaled], axis=0)]
  transfers between devices with their start and end apart: 10 -> 16, of which waited for: 8 -> 8; matrix products, arithmetic and copies ran while one was open for 19% -> 5% of each run, Pallas kernels for 0% -> 0%
where the time goes in v1:
time: 204 us; the launch traced here: 203 us
  Pallas kernels  123 us (60%)
  waiting for transfers between devices  27.9 us (14%)
  starting transfers between devices  27.5 us (13%)
  local copies, waits for them, and re-layouts  13.9 us (7%)
  other arithmetic  10.1 us (5%)
    pallas_call x1, Pallas kernels, smooth_hops(): pl.pallas_call(functools.partial(hop_kernel, parts), out_shape=(jax.Shape...  112 us
    ppermute x15, starting transfers between devices, halving_sum(): got = lax.ppermute(sent, axis, [(i, i ^ 1 << shift) for i in range(size)])  24 us
    ppermute x15, waiting for transfers between devices, halving_sum(): got = lax.ppermute(sent, axis, [(i, i ^ 1 << shift) for i in range(size)])  19.2 us
    pallas_call x1, Pallas kernels, layer_sums(): pl.pallas_call(layer_kernel, out_shape=(jax.ShapeDtypeStruct((4 * width,...  10.9 us
    all_to_all x1, waiting for transfers between devices, on_device(): lax.all_to_all(packed, 'narrow', split_axis=2, concat_axis=1, tiled=True)  8.77 us
    unnamed x23, local copies, waits for them, and re-layouts  6.57 us
    convert_element_type x12, other arithmetic, halving_sum(): term = term.astype(bf16)  5.39 us
  transfers between devices with their start and end apart: 16, of which 8 were waited for; matrix products, arithmetic and copies ran while one was open for 5% of the time, Pallas kernels for 0%

profile of v1, /device:TPU:0, one launch (start us, length us, event | category | flops | bytes accessed | tf_op | source)
XLA Modules:
  0.0 203.0 jit_solution(7913317526460399867)
XLA Ops:
  4.8 111.7 %smooth_hops.1 = (bf16[3,128,4096]{2,1,0:T(8,128)(2,1)}, bf16[4,128,256]{2,1,0:T(8,128)(2,1)}, f32[8,128]{1,0:T(8,128)}) custom-call(s32[32,12]{1,0:T(8,128)} %copy.47.lists, s32[1,8,2]{2,1,0:T(8,128)} %copy.48.sends, bf16[128,4096]{1,0:T(8,128)(2,1)} %feat.1, bf16[32,1536,128]{2,1,0:T(8,128)(2,1)} %bitcast.99, s32[1,256]{1,0:T(1,128)} %bitcast.104, ...), custom_call_target="tpu_custom_call" | custom-call | tf_op jit(solution)/shard_map/smooth_hops/pallas_call | solution.py:179
  119.6 3.5 %all-to-all-start = ((bf16[8,128,4,64]{1,3,0,2:T(8,128)(2,1)}), bf16[8,128,4,64]{1,3,0,2:T(8,128)(2,1)S(1)}, u32[]{:S(2)}, u32[]{:S(2)}) async-start(bf16[8,128,4,64]{1,3,0,2:T(8,128)(2,1)} %copy.50), calls=%async_computation | async-start | bytes 1048576 | tf_op jit(solution)/shard_map/all_to_all | solution.py:377
  123.1 8.8 %all-to-all-done = bf16[8,128,4,64]{1,3,0,2:T(8,128)(2,1)S(1)} async-done(((bf16[8,128,4,64]{1,3,0,2:T(8,128)(2,1)}), bf16[8,128,4,64]{1,3,0,2:T(8,128)(2,1)S(1)}, u32[]{:S(2)}, u32[]{:S(2)}) %all-to-all-start) | async-done | bytes 524320 | tf_op jit(solution)/shard_map/all_to_all | solution.py:377
  132.6 1.5 copy.51
  134.2 10.9 %layer_sums.1 = (bf16[2048,512]{1,0:T(8,128)(2,1)S(1)}, bf16[2048,512]{1,0:T(8,128)(2,1)}, bf16[2048,512]{1,0:T(8,128)(2,1)}) custom-call(bf16[8,512,64]{2,1,0:T(8,128)(2,1)S(1)} %bitcast.97, bf16[512,512]{1,0:T(8,128)(2,1)S(1)} %copy-done, bf16[512,512]{1,0:T(8,128)(2,1)S(1)} %copy-done.1, bf16[512,512]{1,0:T(8,128)(2,1)S(1)} %copy-done.2, ...), custom_call_target="tpu_custom_call" | custom-call | tf_op jit(solution)/shard_map/layer_sums/pallas_call | solution.py:318
  150.8 1.5 fusion.2
  152.8 1.5 fusion.1
  154.4 3.5 %collective-permute-start.6 = (bf16[2,2,2,64,512]{4,3,2,0,1:T(8,128)(2,1)S(1)}, bf16[2,2,2,64,512]{4,3,2,0,1:T(8,128)(2,1)S(1)}, u32[]{:S(2)}, u32[]{:S(2)}) collective-permute-start(bf16[2,2,2,64,512]{4,3,2,0,1:T(8,128)(2,1)S(1)} %dynamic-slice_bitcast_fusion.1), channel_id=1, source_target_pairs={{0,4},{4,0},{8,12},{12,8},{16,20},{20,16},{24,28},{28,24},{1,5},{5... | collective-permute-start | bytes 1572872 | tf_op jit(solution)/shard_map/ppermute | solution.py:350
  157.9 1.5 fusion
  159.5 2.3 %collective-permute-start.11 = (bf16[2,2,2,64,512]{4,3,1,2,0:T(8,128)(2,1)S(1)}, bf16[2,2,2,64,512]{4,3,1,2,0:T(8,128)(2,1)S(1)}, u32[]{:S(2)}, u32[]{:S(2)}) collective-permute-start(bf16[2,2,2,64,512]{4,3,1,2,0:T(8,128)(2,1)S(1)} %dynamic-slice_bitcast_fusion), channel_id=1, source_target_pairs={{0,8},{4,12},{8,0},{12,4},{16,24},{20,28},{24,16},{28,20},{1,9},{5... | collective-permute-start | bytes 1572872 | tf_op jit(solution)/shard_map/ppermute | solution.py:350
  161.8 4.5 %collective-permute-done.1 = bf16[2,2,2,64,512]{4,3,0,1,2:T(8,128)(2,1)S(1)} collective-permute-done((bf16[2,2,2,64,512]{4,3,0,1,2:T(8,128)(2,1)S(1)}, bf16[2,2,2,64,512]{4,3,0,1,2:T(8,128)(2,1)S(1)}, u32[]{:S(2)}, u32[]{:S(2)}) %collective-permute-start.1) | collective-permute-done | bytes 524320 | tf_op jit(solution)/shard_map/ppermute | solution.py:350
  166.5 3.5 %collective-permute-start.2 = (bf16[2,2,64,512]{3,2,0,1:T(8,128)(2,1)S(1)}, bf16[2,2,64,512]{3,2,0,1:T(8,128)(2,1)S(1)}, u32[]{:S(2)}, u32[]{:S(2)}) collective-permute-start(bf16[2,2,64,512]{3,2,0,1:T(8,128)(2,1)S(1)} %dynamic-slice_bitcast_fusion.5), channel_id=1, source_target_pairs={{0,4},{4,0},{8,12},{12,8},{16,20},{20,16},{24,28},{28,24},{1,5},{5... | collective-permute-start | bytes 786440 | tf_op jit(solution)/shard_map/ppermute | solution.py:350
  170.1 2.5 %collective-permute-start.7 = (bf16[2,2,64,512]{3,2,1,0:T(8,128)(2,1)S(1)}, bf16[2,2,64,512]{3,2,1,0:T(8,128)(2,1)S(1)}, u32[]{:S(2)}, u32[]{:S(2)}) collective-permute-start(bf16[2,2,64,512]{3,2,1,0:T(8,128)(2,1)S(1)} %dynamic-slice_bitcast_fusion.4), channel_id=1, source_target_pairs={{0,8},{4,12},{8,0},{12,4},{16,24},{20,28},{24,16},{28,20},{1,9},{5... | collective-permute-start | bytes 786440 | tf_op jit(solution)/shard_map/ppermute | solution.py:350
  172.7 1.6 collective-permute-done.11
  174.5 3.1 %collective-permute-start.12 = (bf16[2,2,64,512]{3,2,0,1:T(8,128)(2,1)S(1)}, bf16[2,2,64,512]{3,2,0,1:T(8,128)(2,1)S(1)}, u32[]{:S(2)}, u32[]{:S(2)}) collective-permute-start(bf16[2,2,64,512]{3,2,0,1:T(8,128)(2,1)S(1)} %dynamic-slice_bitcast_fusion.3), channel_id=1, source_target_pairs={{0,16},{4,20},{8,24},{12,28},{16,0},{20,4},{24,8},{28,12},{1,17},{... | collective-permute-start | bytes 786440 | tf_op jit(solution)/shard_map/ppermute | solution.py:350
  177.7 1.8 collective-permute-start.3
  179.5 5.6 %collective-permute-done.7 = bf16[2,2,64,512]{3,2,1,0:T(8,128)(2,1)S(1)} collective-permute-done((bf16[2,2,64,512]{3,2,1,0:T(8,128)(2,1)S(1)}, bf16[2,2,64,512]{3,2,1,0:T(8,128)(2,1)S(1)}, u32[]{:S(2)}, u32[]{:S(2)}) %collective-permute-start.7) | collective-permute-done | bytes 262176 | tf_op jit(solution)/shard_map/ppermute | solution.py:350
  185.2 1.9 collective-permute-done.12
  187.2 1.9 collective-permute-start.13
  189.1 2.4 %collective-permute-start.4 = (bf16[64,512]{1,0:T(8,128)(2,1)S(1)}, bf16[64,512]{1,0:T(8,128)(2,1)S(1)}, u32[]{:S(2)}, u32[]{:S(2)}) collective-permute-start(bf16[64,512]{1,0:T(8,128)(2,1)S(1)} %dynamic-slice_bitcast_fusion.11), channel_id=1, source_target_pairs={{0,16},{4,20},{8,24},{12,28},{16,0},{20,4},{24,8},{28,12},{1,17},{... | collective-permute-start | bytes 196616 | tf_op jit(solution)/shard_map/ppermute | solution.py:350
  191.5 3.3 %collective-permute-done.8 = bf16[2,64,512]{2,1,0:T(8,128)(2,1)S(1)} collective-permute-done((bf16[2,64,512]{2,1,0:T(8,128)(2,1)S(1)}, bf16[2,64,512]{2,1,0:T(8,128)(2,1)S(1)}, u32[]{:S(2)}, u32[]{:S(2)}) %collective-permute-start.8) | collective-permute-done | bytes 131104 | tf_op jit(solution)/shard_map/ppermute | solution.py:350
  194.9 1.4 collective-permute-start.9
  197.7 1.5 collective-permute-done.9
  201.4 1.7 copy.77
  (74 shorter events, 18.8 us)
Async XLA Ops:
  4.7 112.4 %copy-start.9 = (s32[256,1]{0,1:T(1,128)S(1)}, s32[256,1]{0,1:T(1,128)}, u32[]{:S(2)}) copy-start(s32[256,1]{0,1:T(1,128)} %param.18) | copy-start | bytes 3076
  4.8 112.6 %copy-start.8 = (bf16[4,128,256]{2,1,0:T(8,128)(2,1)S(1)}, bf16[4,128,256]{2,1,0:T(8,128)(2,1)}, u32[]{:S(2)}) copy-start(bf16[4,128,256]{2,1,0:T(8,128)(2,1)} %param.19) | copy-start | bytes 786436
  118.7 15.5 %copy-start = (bf16[512,512]{1,0:T(8,128)(2,1)S(1)}, bf16[512,512]{1,0:T(8,128)(2,1)}, u32[]{:S(2)}) copy-start(bf16[512,512]{1,0:T(8,128)(2,1)} %wq.1) | copy-start | bytes 1572868
  118.7 15.5 %copy-start.1 = (bf16[512,512]{1,0:T(8,128)(2,1)S(1)}, bf16[512,512]{1,0:T(8,128)(2,1)}, u32[]{:S(2)}) copy-start(bf16[512,512]{1,0:T(8,128)(2,1)} %wk.1) | copy-start | bytes 1572868
  118.7 15.5 %copy-start.2 = (bf16[512,512]{1,0:T(8,128)(2,1)S(1)}, bf16[512,512]{1,0:T(8,128)(2,1)}, u32[]{:S(2)}) copy-start(bf16[512,512]{1,0:T(8,128)(2,1)} %wv.1) | copy-start | bytes 1572868
  118.7 15.5 %copy-start.3 = (bf16[512,512]{1,0:T(8,128)(2,1)S(1)}, bf16[512,512]{1,0:T(8,128)(2,1)}, u32[]{:S(2)}) copy-start(bf16[512,512]{1,0:T(8,128)(2,1)} %wo.1) | copy-start | bytes 1572868
  119.6 12.3 %all-to-all-start = ((bf16[8,128,4,64]{1,3,0,2:T(8,128)(2,1)}), bf16[8,128,4,64]{1,3,0,2:T(8,128)(2,1)S(1)}, u32[]{:S(2)}, u32[]{:S(2)}) async-start(bf16[8,128,4,64]{1,3,0,2:T(8,128)(2,1)} %copy.50), calls=%async_computation | async-start | bytes 1048576 | tf_op jit(solution)/shard_map/all_to_all | solution.py:377
  145.3 2.5 %copy-start.5 = (bf16[2048,512]{1,0:T(8,128)(2,1)S(1)}, bf16[2048,512]{1,0:T(8,128)(2,1)}, u32[]{:S(2)}) copy-start(bf16[2048,512]{1,0:T(8,128)(2,1)} %get-tuple-element.14) | copy-start | bytes 6291460
  146.4 4.4 %collective-permute-start = (bf16[2,2,2,2,64,512]{5,4,0,1,2,3:T(8,128)(2,1)}, bf16[2,2,2,2,64,512]{5,4,0,1,2,3:T(8,128)(2,1)}, u32[]{:S(2)}, u32[]{:S(2)}) collective-permute-start(bf16[2,2,2,2,64,512]{5,4,0,1,2,3:T(8,128)(2,1)} %bitcast.96), channel_id=1, source_target_pairs={{0,1},{1,0},{2,3},{3,2},{4,5},{5,4},{6,7},{7,6},{8,9},{9,8},{10,11... | collective-permute-start | bytes 3145736 | tf_op jit(solution)/shard_map/ppermute | solution.py:350
  149.2 3.7 %collective-permute-start.5 = (bf16[2,2,2,2,64,512]{5,4,3,0,1,2:T(8,128)(2,1)}, bf16[2,2,2,2,64,512]{5,4,3,0,1,2:T(8,128)(2,1)}, u32[]{:S(2)}, u32[]{:S(2)}) collective-permute-start(bf16[2,2,2,2,64,512]{5,4,3,0,1,2:T(8,128)(2,1)} %bitcast.95), channel_id=1, source_target_pairs={{0,1},{1,0},{2,3},{3,2},{4,5},{5,4},{6,7},{7,6},{8,9},{9,8},{10,11... | collective-permute-start | bytes 3145736 | tf_op jit(solution)/shard_map/ppermute | solution.py:350
  150.3 7.7 %collective-permute-start.10 = (bf16[2,2,2,2,64,512]{5,4,2,3,0,1:T(8,128)(2,1)}, bf16[2,2,2,2,64,512]{5,4,2,3,0,1:T(8,128)(2,1)}, u32[]{:S(2)}, u32[]{:S(2)}) collective-permute-start(bf16[2,2,2,2,64,512]{5,4,2,3,0,1:T(8,128)(2,1)} %bitcast.94), channel_id=1, source_target_pairs={{0,1},{1,0},{2,3},{3,2},{4,5},{5,4},{6,7},{7,6},{8,9},{9,8},{10,11... | collective-permute-start | bytes 3145736 | tf_op jit(solution)/shard_map/ppermute | solution.py:350
  152.4 13.9 %collective-permute-start.1 = (bf16[2,2,2,64,512]{4,3,0,1,2:T(8,128)(2,1)S(1)}, bf16[2,2,2,64,512]{4,3,0,1,2:T(8,128)(2,1)S(1)}, u32[]{:S(2)}, u32[]{:S(2)}) collective-permute-start(bf16[2,2,2,64,512]{4,3,0,1,2:T(8,128)(2,1)S(1)} %dynamic-slice_bitcast_fusion.2), channel_id=1, source_target_pairs={{0,2},{1,3},{2,0},{3,1},{4,6},{5,7},{6,4},{7,5},{8,10},{9,11},{10,... | collective-permute-start | bytes 1572872 | tf_op jit(solution)/shard_map/ppermute | solution.py:350
  154.4 15.5 %collective-permute-start.6 = (bf16[2,2,2,64,512]{4,3,2,0,1:T(8,128)(2,1)S(1)}, bf16[2,2,2,64,512]{4,3,2,0,1:T(8,128)(2,1)S(1)}, u32[]{:S(2)}, u32[]{:S(2)}) collective-permute-start(bf16[2,2,2,64,512]{4,3,2,0,1:T(8,128)(2,1)S(1)} %dynamic-slice_bitcast_fusion.1), channel_id=1, source_target_pairs={{0,4},{4,0},{8,12},{12,8},{16,20},{20,16},{24,28},{28,24},{1,5},{5... | collective-permute-start | bytes 1572872 | tf_op jit(solution)/shard_map/ppermute | solution.py:350
  159.5 14.8 %collective-permute-start.11 = (bf16[2,2,2,64,512]{4,3,1,2,0:T(8,128)(2,1)S(1)}, bf16[2,2,2,64,512]{4,3,1,2,0:T(8,128)(2,1)S(1)}, u32[]{:S(2)}, u32[]{:S(2)}) collective-permute-start(bf16[2,2,2,64,512]{4,3,1,2,0:T(8,128)(2,1)S(1)} %dynamic-slice_bitcast_fusion), channel_id=1, source_target_pairs={{0,8},{4,12},{8,0},{12,4},{16,24},{20,28},{24,16},{28,20},{1,9},{5... | collective-permute-start | bytes 1572872 | tf_op jit(solution)/shard_map/ppermute | solution.py:350
  166.5 11.1 %collective-permute-start.2 = (bf16[2,2,64,512]{3,2,0,1:T(8,128)(2,1)S(1)}, bf16[2,2,64,512]{3,2,0,1:T(8,128)(2,1)S(1)}, u32[]{:S(2)}, u32[]{:S(2)}) collective-permute-start(bf16[2,2,64,512]{3,2,0,1:T(8,128)(2,1)S(1)} %dynamic-slice_bitcast_fusion.5), channel_id=1, source_target_pairs={{0,4},{4,0},{8,12},{12,8},{16,20},{20,16},{24,28},{28,24},{1,5},{5... | collective-permute-start | bytes 786440 | tf_op jit(solution)/shard_map/ppermute | solution.py:350
  170.1 14.9 %collective-permute-start.7 = (bf16[2,2,64,512]{3,2,1,0:T(8,128)(2,1)S(1)}, bf16[2,2,64,512]{3,2,1,0:T(8,128)(2,1)S(1)}, u32[]{:S(2)}, u32[]{:S(2)}) collective-permute-start(bf16[2,2,64,512]{3,2,1,0:T(8,128)(2,1)S(1)} %dynamic-slice_bitcast_fusion.4), channel_id=1, source_target_pairs={{0,8},{4,12},{8,0},{12,4},{16,24},{20,28},{24,16},{28,20},{1,9},{5... | collective-permute-start | bytes 786440 | tf_op jit(solution)/shard_map/ppermute | solution.py:350
  174.5 12.6 %collective-permute-start.12 = (bf16[2,2,64,512]{3,2,0,1:T(8,128)(2,1)S(1)}, bf16[2,2,64,512]{3,2,0,1:T(8,128)(2,1)S(1)}, u32[]{:S(2)}, u32[]{:S(2)}) collective-permute-start(bf16[2,2,64,512]{3,2,0,1:T(8,128)(2,1)S(1)} %dynamic-slice_bitcast_fusion.3), channel_id=1, source_target_pairs={{0,16},{4,20},{8,24},{12,28},{16,0},{20,4},{24,8},{28,12},{1,17},{... | collective-permute-start | bytes 786440 | tf_op jit(solution)/shard_map/ppermute | solution.py:350
  177.7 23.7 %copy-start.4 = (bf16[3,128,4096]{2,1,0:T(8,128)(2,1)S(1)}, bf16[3,128,4096]{2,1,0:T(8,128)(2,1)}, u32[]{:S(2)}) copy-start(bf16[3,128,4096]{2,1,0:T(8,128)(2,1)} %get-tuple-element.28) | copy-start | bytes 9437188
  177.7 11.4 %collective-permute-start.3 = (bf16[2,64,512]{2,1,0:T(8,128)(2,1)S(1)}, bf16[2,64,512]{2,1,0:T(8,128)(2,1)S(1)}, u32[]{:S(2)}, u32[]{:S(2)}) collective-permute-start(bf16[2,64,512]{2,1,0:T(8,128)(2,1)S(1)} %dynamic-slice_bitcast_fusion.8), channel_id=1, source_target_pairs={{0,8},{4,12},{8,0},{12,4},{16,24},{20,28},{24,16},{28,20},{1,9},{5... | collective-permute-start | bytes 393224 | tf_op jit(solution)/shard_map/ppermute | solution.py:350
  185.1 9.7 %collective-permute-start.8 = (bf16[2,64,512]{2,1,0:T(8,128)(2,1)S(1)}, bf16[2,64,512]{2,1,0:T(8,128)(2,1)S(1)}, u32[]{:S(2)}, u32[]{:S(2)}) collective-permute-start(bf16[2,64,512]{2,1,0:T(8,128)(2,1)S(1)} %dynamic-slice_bitcast_fusion.7), channel_id=1, source_target_pairs={{0,16},{4,20},{8,24},{12,28},{16,0},{20,4},{24,8},{28,12},{1,17},{... | collective-permute-start | bytes 393224 | tf_op jit(solution)/shard_map/ppermute | solution.py:350
  187.2 9.1 %collective-permute-start.13 = (bf16[2,64,512]{2,1,0:T(8,128)(2,1)S(1)}, bf16[2,64,512]{2,1,0:T(8,128)(2,1)S(1)}, u32[]{:S(2)}, u32[]{:S(2)}) collective-permute-start(bf16[2,64,512]{2,1,0:T(8,128)(2,1)S(1)} %dynamic-slice_bitcast_fusion.6), channel_id=1, source_target_pairs={{0,2},{1,3},{2,0},{3,1},{4,6},{5,7},{6,4},{7,5},{8,10},{9,11},{10,... | collective-permute-start | bytes 393224 | tf_op jit(solution)/shard_map/ppermute | solution.py:350
  189.1 7.9 %collective-permute-start.4 = (bf16[64,512]{1,0:T(8,128)(2,1)S(1)}, bf16[64,512]{1,0:T(8,128)(2,1)S(1)}, u32[]{:S(2)}, u32[]{:S(2)}) collective-permute-start(bf16[64,512]{1,0:T(8,128)(2,1)S(1)} %dynamic-slice_bitcast_fusion.11), channel_id=1, source_target_pairs={{0,16},{4,20},{8,24},{12,28},{16,0},{20,4},{24,8},{28,12},{1,17},{... | collective-permute-start | bytes 196616 | tf_op jit(solution)/shard_map/ppermute | solution.py:350
  194.9 4.3 %collective-permute-start.9 = (bf16[64,512]{1,0:T(8,128)(2,1)S(1)}, bf16[64,512]{1,0:T(8,128)(2,1)S(1)}, u32[]{:S(2)}, u32[]{:S(2)}) collective-permute-start(bf16[64,512]{1,0:T(8,128)(2,1)S(1)} %dynamic-slice_bitcast_fusion.10), channel_id=1, source_target_pairs={{0,2},{1,3},{2,0},{3,1},{4,6},{5,7},{6,4},{7,5},{8,10},{9,11},{10,... | collective-permute-start | bytes 196616 | tf_op jit(solution)/shard_map/ppermute | solution.py:350
  196.4 4.3 %collective-permute-start.14 = (bf16[64,512]{1,0:T(8,128)(2,1)S(1)}, bf16[64,512]{1,0:T(8,128)(2,1)S(1)}, u32[]{:S(2)}, u32[]{:S(2)}) collective-permute-start(bf16[64,512]{1,0:T(8,128)(2,1)S(1)} %dynamic-slice_bitcast_fusion.9), channel_id=1, source_target_pairs={{0,4},{4,0},{8,12},{12,8},{16,20},{20,16},{24,28},{28,24},{1,5},{5... | collective-permute-start | bytes 196616 | tf_op jit(solution)/shard_map/ppermute | solution.py:350
  (2 other events, 2.8 us)

commit v2 on v1

v2 whole, which is shorter than its diff:
```python
import functools
import math

import jax
import jax.numpy as jnp
from jax import lax
from jax.experimental import pallas as pl
from jax.experimental.pallas import tpu as pltpu
from jax.sharding import PartitionSpec as P

HEADS = 8
HOPS = 3
TOKS = 4
EPSILON = 1e-05
LANES = 128
MESH = pl.DeviceIdType.MESH
NT = (((1,), (1,)), ((), ()))
TN = (((0,), (0,)), ((), ()))
NN = (((1,), (0,)), ((), ()))
f32 = jnp.float32
bf16 = jnp.bfloat16


def dot(a, b, dims=NN):
    return lax.dot_general(a, b, dims, preferred_element_type=f32)


def hop_kernel(
    parts, narrow, lists, sends, feat, tiles_hbm, ids, owners, cot,
    hops_out, packed_out,
    a_first, a_second, b_first, b_second, fresh_first, fresh_second,
    stage_first, stage_second, tiles, degree, onehot, cnt, cnt_buf, picked, cut, land,
    tile_sem, send_sem, recv_sem, cnt_send, cnt_recv, cut_send, cut_recv,
):
    me = lax.axis_index("wide")
    mine = lax.axis_index("narrow")
    blocks, fan = lists.shape
    slots = sends.shape[2]
    width = feat.shape[0]
    half = width // 2
    rows = ids.shape[1]
    share = rows // narrow
    pool_a = (a_first, a_second)
    pool_b = (b_first, b_second)
    fresh = (fresh_first, fresh_second)
    stage = (stage_first, stage_second)

    load = pltpu.make_async_copy(tiles_hbm, tiles, tile_sem)
    load.start()

    barrier = pltpu.get_barrier_semaphore()

    @pl.loop(1, parts)
    def _(d):
        peer = lax.rem(me + d, parts)
        pl.semaphore_signal(barrier, inc=1, device_id={"wide": peer}, device_id_type=MESH)

    @pl.loop(1, narrow)
    def _(d):
        peer = lax.rem(mine + d, narrow)
        pl.semaphore_signal(barrier, inc=1, device_id={"narrow": peer}, device_id_type=MESH)

    for h in range(2):
        for b in range(blocks):
            block = feat[h * half:(h + 1) * half, b * LANES:(b + 1) * LANES]
            pool_a[h][b] = block
            fresh[h][b] = block
    named = lax.broadcasted_iota(jnp.int32, (cnt.shape[0], rows), 0) == owners[...]
    named = jnp.where(named, 1.0, 0.0)
    cnt[...] = jnp.broadcast_to(jnp.sum(named, axis=1, keepdims=True), cnt.shape)
    pl.semaphore_wait(barrier, parts + narrow - 2)

    def halo_copy(pools, parity, h, dst, src):
        return pltpu.make_async_remote_copy(
            src_ref=stage[h].at[dst],
            dst_ref=pools[h].at[pl.ds(blocks + src * slots, slots)],
            send_sem=send_sem.at[h, dst],
            recv_sem=recv_sem.at[2 * parity + h, src],
            device_id={"wide": dst},
            device_id_type=MESH,
        )

    def count_copy(dst, src):
        return pltpu.make_async_remote_copy(
            src_ref=cnt,
            dst_ref=cnt_buf.at[src],
            send_sem=cnt_send.at[dst],
            recv_sem=cnt_recv.at[src],
            device_id={"wide": dst},
            device_id_type=MESH,
        )

    def cut_copy(piece, dst, src):
        return pltpu.make_async_remote_copy(
            src_ref=cut.at[piece, dst],
            dst_ref=land.at[piece, pl.ds(src * width, width)],
            send_sem=cut_send.at[piece, dst],
            recv_sem=cut_recv.at[piece, src],
            device_id={"narrow": dst},
            device_id_type=MESH,
        )

    def start_halo(pools, parity, h):
        @pl.loop(1, parts)
        def _(d):
            peer = lax.rem(me + d, parts)
            for q in range(slots):
                stage[h][peer, q] = fresh[h][sends[0, peer, q]]
            halo_copy(pools, parity, h, peer, me).start()

        for q in range(slots):
            pools[h][blocks + me * slots + q] = fresh[h][sends[0, me, q]]

    def finish_halo(pools, parity, h):
        @pl.loop(1, parts)
        def _(d):
            peer = lax.rem(me + d, parts)
            halo_copy(pools, parity, h, me, peer).wait_recv()

        @pl.loop(1, parts)
        def _(d):
            peer = lax.rem(me + d, parts)
            halo_copy(pools, parity, h, peer, me).wait_send()

    def start_cut(piece, one, two):
        for n in range(narrow):
            span = slice(n * share, (n + 1) * share)
            cut[piece, n] = jnp.concatenate([one[:, span], two[:, span]], axis=1).astype(bf16)

        @pl.loop(1, narrow)
        def _(d):
            peer = lax.rem(mine + d, narrow)
            cut_copy(piece, peer, mine).start()

        land[piece, pl.ds(mine * width, width), :] = cut[piece, mine]

    def apply(pool, b):
        left = jnp.concatenate([pool[lists[b, k]] for k in range(fan)], axis=1)
        summed = dot(left, tiles[b])
        return (summed / degree[pl.ds(b, 1), :]).astype(bf16)

    for h in range(2):
        start_halo(pool_a, 0, h)

    @pl.loop(1, parts)
    def _(d):
        peer = lax.rem(me + d, parts)
        count_copy(peer, me).start()

    step = onehot.shape[0] // blocks

    @pl.loop(0, blocks)
    def _(b):
        start = pl.multiple_of(b * step, step)
        node = lax.broadcasted_iota(jnp.int32, (step, rows), 0) + start
        onehot[pl.ds(start, step), :] = jnp.where(node == ids[...], 1.0, 0.0).astype(bf16)

    picked[0] = dot(feat[...], onehot[...])
    load.wait()

    @pl.loop(0, blocks)
    def _(b):
        degree[pl.ds(b, 1), :] = jnp.sum(tiles[b].astype(f32), axis=0, keepdims=True)

    cnt_buf[me] = cnt[...]

    @pl.loop(1, parts)
    def _(d):
        peer = lax.rem(me + d, parts)
        count_copy(me, peer).wait_recv()

    counts = jnp.sum(cnt_buf[...], axis=0)[:, 0:1]
    scale = jnp.sum(named * (1.0 / jnp.maximum(counts, 1.0)), axis=0, keepdims=True)
    for pair in range(2):
        start_cut(
            pair,
            cot[2 * pair].astype(f32) * scale,
            cot[2 * pair + 1].astype(f32) * scale,
        )

    unroll = 4

    @pl.loop(0, HOPS)
    def _(hop):
        for h in range(2):
            finish_halo(pool_a, 0, h)

            @pl.loop(0, blocks, step=unroll)
            def _(b):
                for c in range(unroll):
                    once = apply(pool_a[h], b + c)
                    pool_b[h][b + c] = once
                    fresh[h][b + c] = once

            start_halo(pool_b, 1, h)

        for h in range(2):
            finish_halo(pool_b, 1, h)

            @pl.loop(0, blocks, step=unroll)
            def _(b):
                for c in range(unroll):
                    twice = apply(pool_b[h], b + c).astype(f32)
                    smooth = 0.5 * pool_a[h][b + c].astype(f32) + pool_b[h][b + c].astype(f32)
                    smooth = (smooth + twice).astype(bf16)
                    pool_a[h][b + c] = smooth
                    fresh[h][b + c] = smooth
                    start = pl.multiple_of((b + c) * LANES, LANES)
                    hops_out[hop, h * half:(h + 1) * half, pl.ds(start, LANES)] = smooth

            @pl.when(hop < HOPS - 1)
            def _():
                start_halo(pool_a, 0, h)

        picked[hop + 1] = dot(hops_out[hop], onehot[...])

        @pl.when(hop == 0)
        def _():
            start_cut(2, picked[0], picked[1])

    start_cut(3, picked[2], picked[3])

    @pl.loop(1, parts)
    def _(d):
        peer = lax.rem(me + d, parts)
        count_copy(peer, me).wait_send()

    for piece in range(TOKS):
        @pl.loop(1, narrow)
        def _(d):
            peer = lax.rem(mine + d, narrow)
            cut_copy(piece, mine, peer).wait_recv()
            cut_copy(piece, peer, mine).wait_send()

    packed_out[...] = land[...]


def smooth_hops(
    parts, narrow, features, edge_tiles, block_lists, send_lists, train_ids, owners, cotangent
):
    width, nodes = features.shape
    blocks, fan, size, _ = edge_tiles.shape
    slots = send_lists.shape[2]
    rows = train_ids.shape[0]
    pool = blocks + parts * slots
    half = width // 2
    devices = -(-parts * narrow // 8) * 8
    lanes = 2 * rows // narrow
    vmem = pl.BlockSpec(memory_space=pltpu.VMEM)
    smem = pl.BlockSpec(memory_space=pltpu.SMEM)
    return pl.pallas_call(
        functools.partial(hop_kernel, parts, narrow),
        out_shape=(
            jax.ShapeDtypeStruct((HOPS, width, nodes), bf16),
            jax.ShapeDtypeStruct((TOKS, width * narrow, lanes), bf16),
        ),
        in_specs=[smem, smem, vmem, pl.BlockSpec(memory_space=pl.ANY), vmem, vmem, vmem],
        out_specs=(vmem, vmem),
        scratch_shapes=[pltpu.VMEM((pool, half, size), bf16)] * 4
        + [pltpu.VMEM((blocks, half, size), bf16)] * 2
        + [pltpu.VMEM((parts, slots, half, size), bf16)] * 2
        + [
            pltpu.VMEM((blocks, fan * size, size), bf16),
            pltpu.VMEM((blocks, size), f32),
            pltpu.VMEM((nodes, rows), bf16),
            pltpu.VMEM((devices, LANES), f32),
            pltpu.VMEM((parts, devices, LANES), f32),
            pltpu.VMEM((TOKS, width, rows), f32),
            pltpu.VMEM((TOKS, narrow, width, lanes), bf16),
            pltpu.VMEM((TOKS, width * narrow, lanes), bf16),
            pltpu.SemaphoreType.DMA,
            pltpu.SemaphoreType.DMA((2, parts)),
            pltpu.SemaphoreType.DMA((4, parts)),
            pltpu.SemaphoreType.DMA((parts,)),
            pltpu.SemaphoreType.DMA((parts,)),
            pltpu.SemaphoreType.DMA((TOKS, narrow)),
            pltpu.SemaphoreType.DMA((TOKS, narrow)),
        ],
        compiler_params=pltpu.CompilerParams(
            collective_id=0, has_side_effects=True, vmem_limit_bytes=56 * 2**20
        ),
        name="smooth_hops",
    )(
        block_lists, send_lists, features,
        edge_tiles.reshape(blocks, fan * size, size),
        train_ids.reshape(1, rows), owners.reshape(1, rows), cotangent,
    )


def normalize(hidden):
    center = hidden - jnp.mean(hidden, axis=0, keepdims=True)
    inverse = lax.rsqrt(jnp.mean(center * center, axis=0, keepdims=True) + EPSILON)
    return center * inverse, inverse


def layer_kernel(
    bits, orders, packed, wq, wk, wv, wo, wu, wd, attn_out, up_out, down_out,
    nb_ref, cot_ref, g_ref, attn_sum, up_sum, down_sum, attn_in, up_in, down_in,
    send_sem, recv_sem,
):
    outs = (attn_out, up_out, down_out)
    terms = (attn_sum, up_sum, down_sum)
    incoming = (attn_in, up_in, down_in)
    devices, piece = attn_sum.shape[:2]
    stages = len(bits)
    me = [lax.axis_index(axis) for axis, _, _ in bits]
    own = [lax.rem(lax.div(i, 1 << shift), 2) for i, (_, shift, _) in zip(me, bits)]
    partner = [
        {axis: i + (1 - 2 * m) * (1 << shift)} for i, m, (axis, shift, _) in zip(me, own, bits)
    ]
    barrier = pltpu.get_barrier_semaphore()
    for peer in partner:
        pl.semaphore_signal(barrier, inc=1, device_id=peer, device_id_type=MESH)
    pl.semaphore_wait(barrier, stages)

    def place(chain, block):
        spot = 0
        for bit in orders[chain]:
            weight = bits[bit][2]
            if isinstance(block, int):
                spot = 2 * spot + block // weight % 2
            else:
                spot = 2 * spot + lax.rem(lax.div(block, weight), 2)
        return spot

    def put(chain, first, value):
        value = value.astype(bf16)
        for c in range(value.shape[0] // piece):
            terms[chain][place(chain, first + c)] = value[c * piece:(c + 1) * piece, :]

    bases = [[0], [0], [0]]

    def exchange(chain, stage):
        bit = orders[chain][stage]
        half = devices >> (stage + 1)
        base = bases[chain][stage]
        if len(bases[chain]) == stage + 1:
            bases[chain].append(base + own[bit] * half)
        return pltpu.make_async_remote_copy(
            src_ref=terms[chain].at[pl.ds(base + (1 - own[bit]) * half, half)],
            dst_ref=incoming[chain].at[pl.ds(devices - 2 * half, half)],
            send_sem=send_sem.at[chain, stage],
            recv_sem=recv_sem.at[chain, stage],
            device_id=partner[bit],
            device_id_type=MESH,
        )

    def absorb(chain, stage):
        exchange(chain, stage).wait_recv()
        half = devices >> (stage + 1)
        base = bases[chain][stage + 1]

        if stage == stages - 1:
            outs[chain][...] = (
                terms[chain][base].astype(f32) + incoming[chain][devices - 2].astype(f32)
            )
        else:
            @pl.loop(0, half)
            def _(i):
                total = terms[chain][base + i].astype(f32)
                total = total + incoming[chain][devices - 2 * half + i].astype(f32)
                terms[chain][base + i] = total.astype(bf16)

            exchange(chain, stage + 1).start()

    share = packed.shape[2] // 2
    width = packed.shape[1]
    cols = TOKS * share
    head = width // HEADS
    scale = 1.0 / math.sqrt(head)
    cot32 = jnp.concatenate([packed[t].astype(f32) for t in range(2)], axis=1)
    x = jnp.concatenate([packed[2 + t].astype(f32) for t in range(2)], axis=1)
    cot_ref[...] = cot32.astype(bf16)

    def ahead(v, j):
        return v if j == 0 else pltpu.roll(v, cols - j * share, 1)

    def back(v, j):
        return v if j == 0 else pltpu.roll(v, j * share, 1)

    def head_sum(v):
        return jnp.sum(v.reshape(HEADS, head, cols), axis=1)

    def spread(v):
        return jnp.broadcast_to(v[:, None, :], (HEADS, head, cols)).reshape(width, cols)

    def low(v):
        return v.astype(bf16).astype(f32)

    normed_a = normalize(x)[0].astype(bf16)
    query = low(dot(wq[...], normed_a))
    key = low(dot(wk[...], normed_a))
    value = low(dot(wv[...], normed_a))
    scores = [head_sum(query * ahead(key, j)) * scale for j in range(TOKS)]
    top = functools.reduce(jnp.maximum, scores)
    exps = [jnp.exp(s - top) for s in scores]
    total = functools.reduce(jnp.add, exps)
    probs = [e / total for e in exps]
    probs_low = [low(p) for p in probs]
    mixed = functools.reduce(
        jnp.add, [spread(probs_low[j]) * ahead(value, j) for j in range(TOKS)]
    ).astype(bf16)
    residual = low(x + dot(wo[...], mixed))
    second, inverse = normalize(residual)
    nb_ref[...] = second.astype(bf16)
    g_ref[...] = jnp.zeros_like(g_ref)
    chunk = 256
    slope = math.sqrt(2.0 / math.pi)

    @pl.loop(0, wu.shape[0] // chunk)
    def _(i):
        rows = pl.ds(pl.multiple_of(i * chunk, chunk), chunk)
        up = wu[rows, :]
        cot = cot_ref[...]
        normed_b = nb_ref[...]
        pre = dot(up, normed_b)
        square = pre * pre
        tanh = jnp.tanh(slope * (pre + 0.044715 * (square * pre)))
        activated = (0.5 * pre * (1.0 + tanh)).astype(bf16)
        deriv = 0.5 * (1.0 + tanh) + 0.5 * pre * (1.0 - tanh * tanh) * (
            slope * (1.0 + 3.0 * 0.044715 * square)
        )
        put(2, i * (chunk // piece), dot(activated, cot, NT))
        grad_pre = (dot(wd[rows, :], cot) * deriv).astype(bf16)
        put(1, i * (chunk // piece), dot(grad_pre, normed_b, NT))
        g_ref[...] += dot(up, grad_pre, TN)

    exchange(2, 0).start()
    exchange(1, 0).start()
    group = width // piece
    upstream = g_ref[...]
    grad_resid = (
        cot32
        + inverse
        * (
            upstream
            - jnp.mean(upstream, axis=0, keepdims=True)
            - second * jnp.mean(upstream * second, axis=0, keepdims=True)
        )
    ).astype(bf16)
    put(0, 3 * group, dot(grad_resid, mixed, NT))
    grad_mixed = low(dot(wo[...], grad_resid, TN))
    grad_probs = [head_sum(grad_mixed * ahead(value, j)) for j in range(TOKS)]
    grad_value = functools.reduce(
        jnp.add, [back(spread(probs_low[j]) * grad_mixed, j) for j in range(TOKS)]
    ).astype(bf16)
    put(0, 2 * group, dot(grad_value, normed_a, NT))
    inner = functools.reduce(jnp.add, [p * g for p, g in zip(probs, grad_probs)])
    grad_scores = [low(p * (g - inner) * scale) for p, g in zip(probs, grad_probs)]
    grad_query = functools.reduce(
        jnp.add, [spread(grad_scores[j]) * ahead(key, j) for j in range(TOKS)]
    ).astype(bf16)
    put(0, 0, dot(grad_query, normed_a, NT))
    grad_key = functools.reduce(
        jnp.add, [back(spread(grad_scores[j]) * query, j) for j in range(TOKS)]
    ).astype(bf16)
    put(0, group, dot(grad_key, normed_a, NT))
    exchange(0, 0).start()
    for stage in range(stages):
        for chain in (2, 1, 0):
            absorb(chain, stage)
    for chain in range(3):
        for stage in range(stages):
            exchange(chain, stage).wait_send()


def layer_sums(parts, narrow, packed, wq, wk, wv, wo, wu, wd):
    width = packed.shape[1]
    cols = 2 * packed.shape[2]
    devices = parts * narrow
    piece = wu.shape[0] // devices
    bits = [("narrow", s, 1 << s) for s in range(narrow.bit_length() - 1)]
    bits += [("wide", s, narrow << s) for s in range(parts.bit_length() - 1)]
    core, low = 0, narrow.bit_length() - 1
    across = list(range(1, low))
    high = list(range(low + 1, len(bits)))
    orders = (
        [core] + across + [low] + high,
        [core, low] + high + across,
        [core] + high + across + [low],
    )
    vmem = pl.BlockSpec(memory_space=pltpu.VMEM)
    return pl.pallas_call(
        functools.partial(layer_kernel, bits, orders),
        out_shape=(jax.ShapeDtypeStruct((piece, width), f32),) * 3,
        in_specs=[vmem] * 7,
        out_specs=(vmem, vmem, vmem),
        scratch_shapes=[
            pltpu.VMEM((width, cols), bf16),
            pltpu.VMEM((width, cols), bf16),
            pltpu.VMEM((width, cols), f32),
        ]
        + [pltpu.VMEM((devices, piece, width), bf16)] * 6
        + [pltpu.SemaphoreType.DMA((3, len(bits)))] * 2,
        compiler_params=pltpu.CompilerParams(
            collective_id=1, has_side_effects=True, vmem_limit_bytes=48 * 2**20
        ),
        name="layer_sums",
    )(packed, wq, wk, wv, wo, wu, wd)


def on_device(
    features, edge_tiles, block_lists, send_lists, train_ids, owners, cotangent,
    query_weight, key_weight, value_weight, out_weight, up_weight, down_weight,
):
    parts = lax.axis_size("wide")
    narrow = lax.axis_size("narrow")
    hop_tokens, packed = smooth_hops(
        parts, narrow, features, edge_tiles, block_lists, send_lists, train_ids, owners, cotangent
    )
    sums = layer_sums(
        parts, narrow, packed,
        query_weight, key_weight, value_weight, out_weight, up_weight, down_weight,
    )
    return (hop_tokens, *sums)


def solution(mesh):
    in_specs = (
        P("narrow", "wide"),
        P("wide", None, None, None),
        P("wide", None),
        P("wide", None, None),
        P("wide"),
        P("wide", None),
        P(None, "narrow", "wide"),
        P(),
        P(),
        P(),
        P(),
        P(),
        P(),
    )
    out_specs = (
        P(None, "narrow", "wide"),
        P(("wide", "narrow"), None),
        P(("wide", "narrow"), None),
        P(("wide", "narrow"), None),
    )
    return jax.shard_map(
        on_device, mesh=mesh, in_specs=in_specs, out_specs=out_specs, check_vma=False
    )
```

time: 204 us -> 159 us (0.78)
  waiting for transfers between devices: 27.9 us -> 0 us
  starting transfers between devices: 27.5 us -> 0 us
  Pallas kernels: 123 us -> 150 us
  other arithmetic: 10.1 us -> 0 us
  local copies, waits for them, and re-layouts: 13.9 us -> 7.42 us
    pallas_call x2, Pallas kernels: 123 us -> 150 us  [the longest x1 96.4 us: smooth_hops(): pl.pallas_call(functools.partial(hop_kernel, parts, narrow), out_shape=(j...]
    ppermute x15 -> x0, starting transfers between devices: 24 us -> none  [halving_sum(): got = lax.ppermute(sent, axis, [(i, i ^ 1 << shift) for i in range(size)])]
    ppermute x15 -> x0, waiting for transfers between devices: 19.2 us -> none  [halving_sum(): got = lax.ppermute(sent, axis, [(i, i ^ 1 << shift) for i in range(size)])]
    all_to_all x1 -> x0, waiting for transfers between devices: 8.77 us -> none  [on_device(): lax.all_to_all(packed, 'narrow', split_axis=2, concat_axis=1, tiled=True)]
    convert_element_type x13 -> x0, other arithmetic: 5.44 us -> none  [the longest x12 5.39 us: halving_sum(): term = term.astype(bf16)]
    dynamic_slice x5 -> x0, local copies, waits for them, and re-layouts: 3.83 us -> none  [the longest x3 3.25 us: halving_sum(): sent = lax.dynamic_index_in_dim(term, 1 - mine, dim, keepdims=False)]
    all_to_all x1 -> x0, starting transfers between devices: 3.47 us -> none  [on_device(): lax.all_to_all(packed, 'narrow', split_axis=2, concat_axis=1, tiled=True)]
    unnamed x23 -> x20, local copies, waits for them, and re-layouts: 6.57 us -> 7.42 us
  transfers between devices with their start and end apart: 16 -> 0, of which waited for: 8 -> 0; matrix products, arithmetic and copies ran while one was open for 5% -> 0% of each run, Pallas kernels for 0% -> 0%
where the time goes in v2:
time: 159 us; the launch traced here: 158 us
  Pallas kernels  150 us (94%)
  local copies, waits for them, and re-layouts  7.42 us (5%)
    pallas_call x1, Pallas kernels, smooth_hops(): pl.pallas_call(functools.partial(hop_kernel, parts, narrow), out_shape=(j...  96.4 us
    pallas_call x1, Pallas kernels, layer_sums(): pl.pallas_call(functools.partial(layer_kernel, bits, orders), out_shape=(...  53.9 us
    unnamed x20, local copies, waits for them, and re-layouts  7.42 us

profile of v2, /device:TPU:0, one launch (start us, length us, event | category | flops | bytes accessed | tf_op | source)
XLA Modules:
  0.0 158.4 jit_solution(12868453703148063165)
XLA Ops:
  0.6 1.4 copy.17.lists
  2.0 1.3 copy.18.sends
  3.4 0.0 copy-start
  3.4 0.0 copy-start.1
  3.4 0.0 copy-start.2
  3.4 0.0 copy-start.3
  3.4 0.0 copy-start.4
  3.4 96.4 %smooth_hops.1 = (bf16[3,128,4096]{2,1,0:T(8,128)(2,1)}, bf16[4,512,128]{2,1,0:T(8,128)(2,1)}) custom-call(s32[32,12]{1,0:T(8,128)} %copy.17.lists, s32[1,8,2]{2,1,0:T(8,128)} %copy.18.sends, bf16[128,4096]{1,0:T(8,128)(2,1)} %feat.1, bf16[32,1536,128]{2,1,0:T(8,128)(2,1)} %bitcast.3, s32[1,256]{1,0:T(1,128)} %bitcast.4, s32[1,256]{1,0:T(1,128)} %bitcast.5, ...), custom_call_target="tpu_custom_call" | custom-call | tf_op jit(solution)/shard_map/smooth_hops/pallas_call | solution.py:251
  99.8 0.0 copy-done
  99.8 0.0 copy-done.1
  99.8 0.0 copy-done.2
  99.8 0.0 copy-done.3
  99.8 0.0 copy-done.4
  99.8 0.0 copy-start.5
  99.8 1.0 copy-done.5
  100.9 0.0 copy-start.6
  100.9 53.9 %layer_sums.1 = (f32[64,512]{1,0:T(8,128)S(1)}, f32[64,512]{1,0:T(8,128)S(1)}, f32[64,512]{1,0:T(8,128)S(1)}) custom-call(bf16[4,512,128]{2,1,0:T(8,128)(2,1)S(1)} %copy-done.5, bf16[512,512]{1,0:T(8,128)(2,1)S(1)} %copy-done.1, bf16[512,512]{1,0:T(8,128)(2,1)S(1)} %copy-done.2, bf16[512,512]{1,0:T(8,128)(2,1)S(1)} %copy-done.3, ...), custom_call_target="tpu_custom_call" | custom-call | tf_op jit(solution)/shard_map/layer_sums/pallas_call | solution.py:483
  154.8 0.0 copy-done.6
  154.8 1.7 %copy.23 = bf16[3,128,4096]{2,1,0:T(8,128)(2,1)} copy(bf16[3,128,4096]{2,1,0:T(8,128)(2,1)S(1)} %copy-done.6) | data formatting | bytes 6291456
  156.5 0.7 copy.24
  157.1 0.7 copy.25
  157.8 0.7 copy.26
Async XLA Ops:
  3.4 96.4 %copy-start = (bf16[2048,512]{1,0:T(8,128)(2,1)S(1)}, bf16[2048,512]{1,0:T(8,128)(2,1)}, u32[]{:S(2)}) copy-start(bf16[2048,512]{1,0:T(8,128)(2,1)} %wu.1) | copy-start | bytes 6291460
  3.4 96.4 %copy-start.1 = (bf16[512,512]{1,0:T(8,128)(2,1)S(1)}, bf16[512,512]{1,0:T(8,128)(2,1)}, u32[]{:S(2)}) copy-start(bf16[512,512]{1,0:T(8,128)(2,1)} %wq.1) | copy-start | bytes 1572868
  3.4 96.4 %copy-start.2 = (bf16[512,512]{1,0:T(8,128)(2,1)S(1)}, bf16[512,512]{1,0:T(8,128)(2,1)}, u32[]{:S(2)}) copy-start(bf16[512,512]{1,0:T(8,128)(2,1)} %wk.1) | copy-start | bytes 1572868
  3.4 96.5 %copy-start.3 = (bf16[512,512]{1,0:T(8,128)(2,1)S(1)}, bf16[512,512]{1,0:T(8,128)(2,1)}, u32[]{:S(2)}) copy-start(bf16[512,512]{1,0:T(8,128)(2,1)} %wv.1) | copy-start | bytes 1572868
  3.4 96.5 %copy-start.4 = (bf16[512,512]{1,0:T(8,128)(2,1)S(1)}, bf16[512,512]{1,0:T(8,128)(2,1)}, u32[]{:S(2)}) copy-start(bf16[512,512]{1,0:T(8,128)(2,1)} %wo.1) | copy-start | bytes 1572868
  99.8 1.0 copy-start.5
  100.9 53.9 %copy-start.6 = (bf16[3,128,4096]{2,1,0:T(8,128)(2,1)S(1)}, bf16[3,128,4096]{2,1,0:T(8,128)(2,1)}, u32[]{:S(2)}) copy-start(bf16[3,128,4096]{2,1,0:T(8,128)(2,1)} %get-tuple-element.18) | copy-start | bytes 9437188

commit v3 on v2

--- a/solution.py
+++ b/solution.py
@@ -34,8 +34,8 @@
 ):
     me = lax.axis_index("wide")
     mine = lax.axis_index("narrow")
-    blocks, fan = lists.shape
-    slots = sends.shape[2]
+    fan, blocks = lists.shape
+    slots = sends.shape[1]
     width = feat.shape[0]
     half = width // 2
     rows = ids.shape[1]
@@ -105,11 +105,11 @@
         def _(d):
             peer = lax.rem(me + d, parts)
             for q in range(slots):
-                stage[h][peer, q] = fresh[h][sends[0, peer, q]]
+                stage[h][peer, q] = fresh[h][sends[0, q, peer]]
             halo_copy(pools, parity, h, peer, me).start()
 
         for q in range(slots):
-            pools[h][blocks + me * slots + q] = fresh[h][sends[0, me, q]]
+            pools[h][blocks + me * slots + q] = fresh[h][sends[0, q, me]]
 
     def finish_halo(pools, parity, h):
         @pl.loop(1, parts)
@@ -135,7 +135,7 @@
         land[piece, pl.ds(mine * width, width), :] = cut[piece, mine]
 
     def apply(pool, b):
-        left = jnp.concatenate([pool[lists[b, k]] for k in range(fan)], axis=1)
+        left = jnp.concatenate([pool[lists[k, b]] for k in range(fan)], axis=1)
         summed = dot(left, tiles[b])
         return (summed / degree[pl.ds(b, 1), :]).astype(bf16)
 
@@ -281,7 +281,7 @@
         ),
         name="smooth_hops",
     )(
-        block_lists, send_lists, features,
+        block_lists.T, send_lists.transpose(0, 2, 1), features,
         edge_tiles.reshape(blocks, fan * size, size),
         train_ids.reshape(1, rows), owners.reshape(1, rows), cotangent,
     )
@@ -471,14 +471,8 @@
     piece = wu.shape[0] // devices
     bits = [("narrow", s, 1 << s) for s in range(narrow.bit_length() - 1)]
     bits += [("wide", s, narrow << s) for s in range(parts.bit_length() - 1)]
-    core, low = 0, narrow.bit_length() - 1
-    across = list(range(1, low))
-    high = list(range(low + 1, len(bits)))
-    orders = (
-        [core] + across + [low] + high,
-        [core, low] + high + across,
-        [core] + high + across + [low],
-    )
+    near, far = list(range(1, min(4, len(bits)))), list(range(4, len(bits)))
+    orders = [[0] + near[c:] + near[:c] + far for c in range(3)]
     vmem = pl.BlockSpec(memory_space=pltpu.VMEM)
     return pl.pallas_call(
         functools.partial(layer_kernel, bits, orders),

time: 159 us -> 153 us (0.962)
  local copies, waits for them, and re-layouts: 7.42 us -> 4.69 us
  Pallas kernels: 150 us -> 148 us
    unnamed x20 -> x18, local copies, waits for them, and re-layouts: 7.42 us -> 4.69 us
    pallas_call x1, Pallas kernels: 53.9 us -> 51.3 us  [layer_sums(): pl.pallas_call(functools.partial(layer_kernel, bits, orders), out_shape=(...]
where the time goes in v3:
time: 153 us
  Pallas kernels  148 us (97%)
  local copies, waits for them, and re-layouts  4.69 us (3%)
    pallas_call x1, Pallas kernels, smooth_hops(): pl.pallas_call(functools.partial(hop_kernel, parts, narrow), out_shape=(j...  96.4 us
    pallas_call x1, Pallas kernels, layer_sums(): pl.pallas_call(functools.partial(layer_kernel, bits, orders), out_shape=(...  51.3 us
    unnamed x18, local copies, waits for them, and re-layouts  4.69 us

profile of v3, /device:TPU:0, one launch (start us, length us, event | category | flops | bytes accessed | tf_op | source)
XLA Modules:
  0.0 153.2 jit_solution(16414497307912944202)
XLA Ops:
  0.6 0.0 copy-start
  0.6 0.0 copy-start.1
  0.7 0.0 copy-start.2
  0.7 0.0 copy-start.3
  0.7 0.0 copy-start.4
  0.7 96.4 %smooth_hops.1 = (bf16[3,128,4096]{2,1,0:T(8,128)(2,1)}, bf16[4,512,128]{2,1,0:T(8,128)(2,1)}) custom-call(s32[12,32]{1,0:T(8,128)} %bitcast.6, s32[1,2,8]{2,1,0:T(2,128)} %bitcast.7, bf16[128,4096]{1,0:T(8,128)(2,1)} %feat.1, bf16[32,1536,128]{2,1,0:T(8,128)(2,1)} %bitcast.5, s32[1,256]{1,0:T(1,128)} %bitcast.8, s32[1,256]{1,0:T(1,128)} %bitcast.9, ...), custom_call_target="tpu_custom_call" | custom-call | tf_op jit(solution)/shard_map/smooth_hops/pallas_call | solution.py:251
  97.1 0.0 copy-done
  97.1 0.0 copy-done.1
  97.1 0.0 copy-done.2
  97.1 0.0 copy-done.3
  97.1 0.0 copy-done.4
  97.2 0.0 copy-start.5
  97.2 1.0 copy-done.5
  98.2 0.0 copy-start.6
  98.2 51.3 %layer_sums.1 = (f32[64,512]{1,0:T(8,128)S(1)}, f32[64,512]{1,0:T(8,128)S(1)}, f32[64,512]{1,0:T(8,128)S(1)}) custom-call(bf16[4,512,128]{2,1,0:T(8,128)(2,1)S(1)} %copy-done.5, bf16[512,512]{1,0:T(8,128)(2,1)S(1)} %copy-done.1, bf16[512,512]{1,0:T(8,128)(2,1)S(1)} %copy-done.2, bf16[512,512]{1,0:T(8,128)(2,1)S(1)} %copy-done.3, ...), custom_call_target="tpu_custom_call" | custom-call | tf_op jit(solution)/shard_map/layer_sums/pallas_call | solution.py:477
  149.5 0.0 copy-done.6
  149.5 1.7 %copy.21 = bf16[3,128,4096]{2,1,0:T(8,128)(2,1)} copy(bf16[3,128,4096]{2,1,0:T(8,128)(2,1)S(1)} %copy-done.6) | data formatting | bytes 6291456
  151.2 0.7 copy.22
  151.9 0.7 copy.23
  152.5 0.7 copy.24
Async XLA Ops:
  0.6 96.5 %copy-start = (bf16[2048,512]{1,0:T(8,128)(2,1)S(1)}, bf16[2048,512]{1,0:T(8,128)(2,1)}, u32[]{:S(2)}) copy-start(bf16[2048,512]{1,0:T(8,128)(2,1)} %wu.1) | copy-start | bytes 6291460
  0.6 96.5 %copy-start.1 = (bf16[512,512]{1,0:T(8,128)(2,1)S(1)}, bf16[512,512]{1,0:T(8,128)(2,1)}, u32[]{:S(2)}) copy-start(bf16[512,512]{1,0:T(8,128)(2,1)} %wq.1) | copy-start | bytes 1572868
  0.7 96.5 %copy-start.2 = (bf16[512,512]{1,0:T(8,128)(2,1)S(1)}, bf16[512,512]{1,0:T(8,128)(2,1)}, u32[]{:S(2)}) copy-start(bf16[512,512]{1,0:T(8,128)(2,1)} %wk.1) | copy-start | bytes 1572868
  0.7 96.5 %copy-start.3 = (bf16[512,512]{1,0:T(8,128)(2,1)S(1)}, bf16[512,512]{1,0:T(8,128)(2,1)}, u32[]{:S(2)}) copy-start(bf16[512,512]{1,0:T(8,128)(2,1)} %wv.1) | copy-start | bytes 1572868
  0.7 96.5 %copy-start.4 = (bf16[512,512]{1,0:T(8,128)(2,1)S(1)}, bf16[512,512]{1,0:T(8,128)(2,1)}, u32[]{:S(2)}) copy-start(bf16[512,512]{1,0:T(8,128)(2,1)} %wo.1) | copy-start | bytes 1572868
  97.2 1.0 copy-start.5
  98.2 51.3 %copy-start.6 = (bf16[3,128,4096]{2,1,0:T(8,128)(2,1)S(1)}, bf16[3,128,4096]{2,1,0:T(8,128)(2,1)}, u32[]{:S(2)}) copy-start(bf16[3,128,4096]{2,1,0:T(8,128)(2,1)} %get-tuple-element.18) | copy-start | bytes 9437188
